TPU v7x, 32 devices: a whole 2x2x4 slice. The times are simulated.
32 devices in a mesh: clip: 8 (over z, core), frame: 4 (over y, x).
Axes of the slice: x: 2, y: 2, z: 4, core: 2. Of those that a mesh axis runs over, the one named last changes fastest.
Arguments:
- block_input: bfloat16 [16, 16, 64, 1152], P('clip', 'frame'), may hold values from -6 to 6
- modulation: bfloat16 [16, 6912], P('clip'), may hold values from -4 to 4
- frame_counts: int32 [16], P('clip'), may hold values from 8 to 16, as said below
- qkv_weight: bfloat16 [1152, 3456], replicated, may hold values from -0.1875 to 0.1875
- qv_bias: bfloat16 [2304], replicated, may hold values from -3 to 3
- out_weight: bfloat16 [1152, 1152], replicated, may hold values from -0.375 to 0.375
- out_bias: bfloat16 [1152], replicated, may hold values from -3 to 3
- fc1_weight: bfloat16 [1152, 4608], replicated, may hold values from -0.1875 to 0.1875
- fc1_bias: bfloat16 [4608], replicated, may hold values from -3 to 3
- fc2_weight: bfloat16 [4608, 1152], replicated, may hold values from -0.09375 to 0.09375
- fc2_bias: bfloat16 [1152], replicated, may hold values from -3 to 3
- out_cotangent: bfloat16 [16, 16, 64, 1152], P('clip', 'frame'), may hold values from -6 to 6
Outputs:
- block_output: bfloat16 [16, 16, 64, 1152], P('clip', 'frame')
- input_grad: bfloat16 [16, 16, 64, 1152], P('clip', 'frame')
- modulation_grad: float32 [16, 6912], P('clip', 'frame')
- qkv_weight_grad: float32 [1152, 3456], P('clip', 'frame')
- qv_bias_grad: float32 [2304], P('frame')
- out_weight_grad: float32 [1152, 1152], P('clip', 'frame')
- out_bias_grad: float32 [1152], P('frame')
- fc1_weight_grad: float32 [1152, 4608], P('clip', 'frame')
- fc1_bias_grad: float32 [4608], P('frame')
- fc2_weight_grad: float32 [4608, 1152], P('clip', 'frame')
- fc2_bias_grad: float32 [1152], P('frame')
Inputs may be any that keep to these rules, and one draw needn't show every extreme that they name: `frame_counts`: each clip holds 8 to 16 frames in its leading slots; some clip holds 16 and some other clip 16 // 2.
All inputs are finite; a program needn't handle non-finite values.
Results may differ from a plain program's by a relative error of at most 0.013.
The roundings to bfloat16 on the way count: a program that leaves them out, or rounds other values in their place, can miss the bound.
Values may be sent and summed in bfloat16 or wider, within the bound.
A program may use at most 256 MiB of HBM per device.

v0:
```python
import jax
import jax.numpy as jnp
from jax import lax
from jax.sharding import PartitionSpec as P

HEADS = 16


EPSILON = 1e-06
NEGATIVE = -1e30


def normalize(values):
    centred = values - jnp.mean(values, axis=-1, keepdims=True)
    variance = jnp.mean(centred * centred, axis=-1, keepdims=True)
    return centred * lax.rsqrt(variance + EPSILON)


def modulate(values, shift_term, scale_term):
    return normalize(values) * (1.0 + scale_term) + shift_term


def gelu_tanh(inputs):
    return jax.nn.gelu(inputs, approximate=True)


def contract_rows(left, right):
    return lax.dot_general(
        left, right, (((0,), (0,)), ((), ())), preferred_element_type=jnp.float32
    )


def contract_cols(left, right):
    return lax.dot_general(
        left, right, (((1,), (1,)), ((), ())), preferred_element_type=jnp.float32
    )


def on_device(
    block_input,
    modulation,
    frame_counts,
    qkv_weight,
    qv_bias,
    out_weight,
    out_bias,
    fc1_weight,
    fc1_bias,
    fc2_weight,
    fc2_bias,
    out_cotangent,
):
    swapped = lax.all_to_all(block_input, "frame", split_axis=2, concat_axis=1, tiled=True)
    clip_count, frames, patches, model_width = swapped.shape
    head_width = model_width // HEADS
    row_count = clip_count * frames * patches
    factor = head_width ** (-0.5)
    frame_valid = (jnp.arange(frames)[None, :] < frame_counts[:, None]).astype(jnp.float32)
    valid_rows = frame_valid[:, :, None, None]
    key_valid = frame_valid[:, None, None, None, :] > 0.5
    modulators = modulation.astype(jnp.float32).reshape(clip_count, 6, model_width)[
        :, :, None, None, :
    ]
    shift_one = modulators[:, 0]
    scale_one = modulators[:, 1]
    gate_one = modulators[:, 2]
    shift_two = modulators[:, 3]
    scale_two = modulators[:, 4]
    gate_two = modulators[:, 5]
    residual = swapped.astype(jnp.float32)
    normed_full, modulate_back_one = jax.vjp(modulate, residual, shift_one, scale_one)
    normed_one = normed_full.astype(jnp.bfloat16).reshape(row_count, model_width)
    bias_full = jnp.concatenate(
        [qv_bias[:model_width], jnp.zeros((model_width,), jnp.bfloat16), qv_bias[model_width:]]
    ).astype(jnp.float32)
    projected = (
        jnp.dot(normed_one, qkv_weight, preferred_element_type=jnp.float32) + bias_full
    ).astype(jnp.bfloat16)
    shaped = projected.reshape(clip_count, frames, patches, 3, HEADS, head_width)
    queries = shaped[:, :, :, 0]
    keys_all = shaped[:, :, :, 1]
    values_all = shaped[:, :, :, 2]
    scores = (
        jnp.einsum("cfphd,cgphd->cphfg", queries, keys_all, preferred_element_type=jnp.float32)
        * factor
    )
    scores = jnp.where(key_valid, scores, NEGATIVE)
    row_peak = jnp.max(scores, axis=-1, keepdims=True)
    exponent = jnp.exp(scores - row_peak)
    attention_weights = exponent / jnp.sum(exponent, axis=-1, keepdims=True)
    weights_low = attention_weights.astype(jnp.bfloat16)
    context = jnp.einsum(
        "cphfg,cgphd->cfphd", weights_low, values_all, preferred_element_type=jnp.float32
    )
    context_low = context.astype(jnp.bfloat16).reshape(row_count, model_width)
    attended = jnp.dot(
        context_low, out_weight, preferred_element_type=jnp.float32
    ) + out_bias.astype(jnp.float32)
    attended = attended.reshape(clip_count, frames, patches, model_width)
    middle = residual + gate_one * attended
    normed_mid, modulate_back_two = jax.vjp(modulate, middle, shift_two, scale_two)
    normed_two = normed_mid.astype(jnp.bfloat16).reshape(row_count, model_width)
    hidden = jnp.dot(normed_two, fc1_weight, preferred_element_type=jnp.float32) + fc1_bias.astype(
        jnp.float32
    )
    activated_full, gelu_back = jax.vjp(gelu_tanh, hidden)
    activated = activated_full.astype(jnp.bfloat16)
    branch_two = jnp.dot(
        activated, fc2_weight, preferred_element_type=jnp.float32
    ) + fc2_bias.astype(jnp.float32)
    branch_two = branch_two.reshape(clip_count, frames, patches, model_width)
    result = valid_rows * (middle + gate_two * branch_two)
    block_output = lax.all_to_all(
        result.astype(jnp.bfloat16), "frame", split_axis=1, concat_axis=2, tiled=True
    )
    cotangent = lax.all_to_all(
        out_cotangent, "frame", split_axis=2, concat_axis=1, tiled=True
    ).astype(jnp.float32)
    d_result = valid_rows * cotangent
    d_gate_two = jnp.sum(d_result * branch_two, axis=(1, 2))
    d_branch = (d_result * gate_two).astype(jnp.bfloat16).reshape(row_count, model_width)
    d_fc2_bias = jnp.sum(d_branch.astype(jnp.float32), axis=0)
    d_fc2_weight = contract_rows(activated, d_branch)
    d_activated = contract_cols(d_branch, fc2_weight)
    d_hidden = gelu_back(d_activated)[0].astype(jnp.bfloat16)
    d_fc1_bias = jnp.sum(d_hidden.astype(jnp.float32), axis=0)
    d_fc1_weight = contract_rows(normed_two, d_hidden)
    d_normed_two = contract_cols(d_hidden, fc1_weight).reshape(
        clip_count, frames, patches, model_width
    )
    d_middle_norm, d_shift_two, d_scale_two = modulate_back_two(d_normed_two)
    d_middle = d_result + d_middle_norm
    d_gate_one = jnp.sum(d_middle * attended, axis=(1, 2))
    d_attended = (d_middle * gate_one).astype(jnp.bfloat16).reshape(row_count, model_width)
    d_out_bias = jnp.sum(d_attended.astype(jnp.float32), axis=0)
    d_out_weight = contract_rows(context_low, d_attended)
    d_context = contract_cols(d_attended, out_weight).astype(jnp.bfloat16)
    d_context = d_context.reshape(clip_count, frames, patches, HEADS, head_width)
    d_weights = jnp.einsum(
        "cfphd,cgphd->cphfg", d_context, values_all, preferred_element_type=jnp.float32
    )
    d_values = jnp.einsum(
        "cphfg,cfphd->cgphd", weights_low, d_context, preferred_element_type=jnp.float32
    )
    d_scores = attention_weights * (
        d_weights - jnp.sum(attention_weights * d_weights, axis=-1, keepdims=True)
    )
    d_scores = d_scores.astype(jnp.bfloat16)
    d_queries = (
        jnp.einsum("cphfg,cgphd->cfphd", d_scores, keys_all, preferred_element_type=jnp.float32)
        * factor
    )
    d_keys = (
        jnp.einsum("cphfg,cfphd->cgphd", d_scores, queries, preferred_element_type=jnp.float32)
        * factor
    )
    d_projected = (
        jnp.stack([d_queries, d_keys, d_values], axis=3)
        .astype(jnp.bfloat16)
        .reshape(row_count, 3 * model_width)
    )
    column_sums = jnp.sum(d_projected.astype(jnp.float32), axis=0)
    d_qv_bias = jnp.concatenate([column_sums[:model_width], column_sums[2 * model_width :]])
    d_qkv_weight = contract_rows(normed_one, d_projected)
    d_normed_one = contract_cols(d_projected, qkv_weight).reshape(
        clip_count, frames, patches, model_width
    )
    d_residual, d_shift_one, d_scale_one = modulate_back_one(d_normed_one)
    d_input = d_middle + d_residual
    input_grad = lax.all_to_all(
        d_input.astype(jnp.bfloat16), "frame", split_axis=1, concat_axis=2, tiled=True
    )
    d_modulation = jnp.stack(
        [
            d_shift_one.reshape(clip_count, model_width),
            d_scale_one.reshape(clip_count, model_width),
            d_gate_one,
            d_shift_two.reshape(clip_count, model_width),
            d_scale_two.reshape(clip_count, model_width),
            d_gate_two,
        ],
        axis=1,
    ).reshape(clip_count, 6 * model_width)
    every_part = (
        lax.psum_scatter(d_qkv_weight, "frame", scatter_dimension=1, tiled=True),
        lax.psum_scatter(d_out_weight, "frame", scatter_dimension=1, tiled=True),
        lax.psum_scatter(d_fc1_weight, "frame", scatter_dimension=1, tiled=True),
        lax.psum_scatter(d_fc2_weight, "frame", scatter_dimension=1, tiled=True),
        lax.psum_scatter(d_modulation, "frame", scatter_dimension=1, tiled=True),
        lax.psum_scatter(d_qv_bias, "frame", scatter_dimension=0, tiled=True),
        lax.psum_scatter(d_out_bias, "frame", scatter_dimension=0, tiled=True),
        lax.psum_scatter(d_fc1_bias, "frame", scatter_dimension=0, tiled=True),
        lax.psum_scatter(d_fc2_bias, "frame", scatter_dimension=0, tiled=True),
    )
    every_mat = (
        lax.psum_scatter(every_part[0], "clip", scatter_dimension=0, tiled=True),
        lax.psum_scatter(every_part[1], "clip", scatter_dimension=0, tiled=True),
        lax.psum_scatter(every_part[2], "clip", scatter_dimension=0, tiled=True),
        lax.psum_scatter(every_part[3], "clip", scatter_dimension=0, tiled=True),
    )
    qkv_grad = every_mat[0]
    out_grad = every_mat[1]
    fc1_grad = every_mat[2]
    fc2_grad = every_mat[3]
    modulation_grad = every_part[4]
    bias_parts = (every_part[5], every_part[6], every_part[7], every_part[8])
    bias_totals = lax.psum((bias_parts[0], bias_parts[1], bias_parts[2], bias_parts[3]), "clip")
    return (
        block_output,
        input_grad,
        modulation_grad,
        qkv_grad,
        bias_totals[0],
        out_grad,
        bias_totals[1],
        fc1_grad,
        bias_totals[2],
        fc2_grad,
        bias_totals[3],
    )


def solution(mesh):
    placed = (
        P("clip", "frame", None, None),
        P("clip", None),
        P("clip"),
        P(),
        P(),
        P(),
        P(),
        P(),
        P(),
        P(),
        P(),
        P("clip", "frame", None, None),
    )
    return jax.shard_map(
        on_device,
        mesh=mesh,
        in_specs=placed,
        out_specs=(
            P("clip", "frame", None, None),
            P("clip", "frame", None, None),
            P("clip", "frame"),
            P("clip", "frame"),
            P("frame"),
            P("clip", "frame"),
            P("frame"),
            P("clip", "frame"),
            P("frame"),
            P("clip", "frame"),
            P("frame"),
        ),
        check_vma=False,
    )
```

profile of v0, /device:TPU:0, one launch (start us, length us, event | category | flops | bytes accessed | tf_op | source)
XLA Modules:
  0.0 1028.3 jit_solution(13910262976260021615)
XLA Ops:
  7.2 3.3 copy.57
  10.6 5.3 all-to-all-start
  16.1 3.2 copy.66
  19.6 12.0 %all-to-all-done = bf16[2,4,64,1152]{3,1,0,2:T(4,128)(2,1)} async-done(((bf16[2,4,64,1152]{3,1,0,2:T(4,128)(2,1)}), bf16[2,4,64,1152]{3,1,0,2:T(4,128)(2,1)}, u32[]{:S(2)}, u32[]{:S(2)}) %all-to-all-start) | async-done | bytes 1179680 | tf_op jit(solution)/shard_map/all_to_all | solution.py:53
  31.6 4.3 all-to-all-start.2
  43.7 10.0 add_convert_fusion
  53.8 13.6 %reshape.417 = bf16[2,16,16,3,16,72]{5,4,3,2,1,0:T(8,128)(2,1)} reshape(bf16[512,3456]{1,0:T(8,128)(2,1)} %add_convert_fusion) | data formatting | bytes 7077888 | tf_op jit(solution)/shard_map/reshape | solution.py:79
  67.4 5.0 fusion.48
  72.4 2.5 fusion.33
  74.9 2.4 fusion.52
  77.3 1.8 convert_bitcast_fusion
  79.2 1.9 copy.63
  81.1 5.1 reshape.418
  86.2 3.3 convolution_add_fusion.1
  89.5 2.2 fusion.47
  91.7 2.0 multiply_reduce_fusion.6
  93.9 1.6 copy.67
  95.9 2.9 fusion.17
  98.9 9.5 fusion.53
  108.7 3.4 copy-done.47
  113.1 10.3 %fusion.42 = f32[4608,1152]{0,1:T(8,128)} fusion(bf16[512,1152]{1,0:T(8,128)(2,1)S(1)} %fusion.19, f32[512,4608]{1,0:T(8,128)S(1)} %fusion.53, f32[4608]{0:T(1024)S(1)} %convert_element_type.207), kind=kOutput, calls=%fused_computation.115 | convolution fusion | flops 5459410944 | bytes 31868928 | tf_op jit(solution)/shard_map/dot_general | solution.py:28
  124.1 15.8 %convert_reduce_fusion.1 = (f32[4608]{0:T(1024)S(1)}, bf16[512,4608]{1,0:T(8,128)(2,1)S(1)}) fusion(f32[512,4608]{1,0:T(8,128)} %copy-done.47, f32[4608]{0:T(1024)S(1)} %convert_element_type.207, bf16[512,1152]{1,0:T(8,128)(2,1)} %copy-done.33, bf16[4608,1152]{1,0:T(8,128)(2,1)} %param.21), kind=kOutput, calls=%fused_computation.12 | convolution fusion | flops 5490077184 | bytes 25989120 | tf_op jit(solution)/shard_map/dot_general | solution.py:34
  139.9 11.1 %fusion.54 = f32[512,1152]{1,0:T(8,128)S(1)} fusion(bf16[512,4608]{1,0:T(8,128)(2,1)S(1)} %get-tuple-element.58, bf16[1152,4608]{1,0:T(8,128)(2,1)} %param.19), kind=kOutput, calls=%fused_computation.126 | convolution fusion | flops 5435817984 | bytes 17694720 | tf_op jit(solution)/shard_map/dot_general | solution.py:34
  153.0 4.3 fusion.46
  158.9 4.1 fusion.56
  163.0 4.2 convolution_convert_fusion
  167.3 5.2 reshape.424
  172.5 7.1 multiply_reduce_fusion
  181.3 1.7 multiply_bitcast_fusion.1
  183.2 1.7 multiply_bitcast_fusion
  184.9 1.6 convolution_bitcast_fusion
  186.5 2.2 convert_reduce_fusion
  188.7 4.2 copy.71
  193.0 11.3 %convert_element_type.223 = bf16[2,16,16,3456]{3,2,1,0:T(8,128)(2,1)} reshape(bf16[2,16,16,3,16,72]{5,4,3,2,1,0:T(8,128)(2,1)} %copy.71) | data formatting | bytes 7077888 | tf_op jit(solution)/shard_map/convert_element_type | solution.py:159
  204.3 11.0 %convert_element_type.227 = bf16[512,3456]{1,0:T(8,128)(2,1)} reshape(bf16[2,16,16,3,16,72]{5,4,3,2,1,0:T(8,128)(2,1)} %copy.71) | data formatting | bytes 7077888 | tf_op jit(solution)/shard_map/convert_element_type | solution.py:159
  215.3 9.8 multiply_reduce_fusion.4
  225.2 2.0 multiply_reduce_fusion.3
  227.2 13.6 %convolution_add_fusion = f32[512,1152]{1,0:T(8,128)S(1)} fusion(bf16[4608,1152]{1,0:T(8,128)(2,1)} %param.21, f32[1152]{0:T(1024)S(1)} %convert_element_type.209, f32[512,4608]{1,0:T(8,128)} %copy-done.47, f32[4608]{0:T(1024)S(1)} %convert_element_type.207), kind=kOutput, calls=%fused_computation.30 | convolution fusion | flops 5460000768 | bytes 22436352 | tf_op jit(solution)/shard_map/dot_general | solution.py:108
  240.9 2.7 multiply_reduce_fusion.2
  243.6 2.1 add_convert_fusion.1
  245.8 8.4 fusion.55
  255.8 12.2 %fusion.57 = f32[1152,4608]{1,0:T(8,128)} fusion(bf16[512,1152]{1,0:T(8,128)(2,1)S(1)} %copy-done.23, bf16[512,4608]{1,0:T(8,128)(2,1)} %copy-done.21), kind=kOutput, calls=%fused_computation.129 | convolution fusion | flops 5435817984 | bytes 27131904 | tf_op jit(solution)/shard_map/dot_general | solution.py:28
  268.3 2.7 copy.88
  271.0 44.4 %reduce-scatter.26.cloned.1.call-done = f32[4608,288]{0,1:T(8,128)} async-done(((f32[4608,1152]{0,1:T(8,128)}), f32[4608,288]{0,1:T(8,128)}) %reduce-scatter.26.cloned.1.call-update) | async-done | bytes 5308432 | tf_op jit(solution)/shard_map/reduce_scatter | solution.py:188
  315.4 6.7 copy.86
  322.2 58.5 %reduce-scatter.20.cloned.1.call-done = f32[1152,288]{0,1:T(8,128)} async-done(((f32[1152,1152]{0,1:T(8,128)}), f32[1152,288]{0,1:T(8,128)}) %reduce-scatter.20.cloned.1.call-update) | async-done | bytes 1327120 | tf_op jit(solution)/shard_map/reduce_scatter | solution.py:186
  380.7 3.1 copy.84
  383.9 147.6 %reduce-scatter.18.cloned.1.call-done = f32[1152,864]{0,1:T(8,128)} async-done(((f32[1152,3456]{0,1:T(8,128)}), f32[1152,864]{0,1:T(8,128)}) %reduce-scatter.18.cloned.1.call-update) | async-done | bytes 3981328 | tf_op jit(solution)/shard_map/reduce_scatter | solution.py:185
  531.5 5.6 copy.82
  537.1 187.3 %reduce-scatter.22.cloned.1.call-done = f32[1152,1152]{1,0:T(8,128)} async-done(((f32[1152,4608]{1,0:T(8,128)}), f32[1152,1152]{1,0:T(8,128)}) %reduce-scatter.22.cloned.1.call-update) | async-done | bytes 5308432 | tf_op jit(solution)/shard_map/reduce_scatter | solution.py:187
  726.8 3.5 all-to-all-start.3
  734.2 21.7 %all-to-all-done.3 = bf16[2,16,16,1152]{3,2,0,1:T(8,128)(2,1)S(1)} async-done(((bf16[2,16,16,1152]{3,2,0,1:T(8,128)(2,1)}), bf16[2,16,16,1152]{3,2,0,1:T(8,128)(2,1)S(1)}, u32[]{:S(2)}, u32[]{:S(2)}) %all-to-all-start.3) | async-done | bytes 1179680 | tf_op jit(solution)/shard_map/all_to_all | solution.py:170
  755.9 4.3 all-to-all-start.1
  760.2 1.6 bitcast_convert_fusion
  762.4 25.4 %all-reduce.5 = (f32[2304]{0:T(1024)S(1)}, f32[1152]{0:T(1024)S(1)}, f32[4608]{0:T(1024)S(1)}, f32[1152]{0:T(1024)S(1)}) all-reduce(f32[2304]{0:T(1024)S(1)} %pad_maximum_fusion, f32[1152]{0:T(1024)S(1)} %get-tuple-element.59, f32[4608]{0:T(1024)S(1)} %get-tuple-element.57, ...), channel_id=5, replica_groups=mesh['clip'=8,'frame'=4] {'frame'}, use_global_device_ids=true, to_apply=%region_21.22.clone | all-reduce | flops 9216 | bytes 73728
  788.2 26.7 %all-reduce.4 = (f32[576]{0:T(1024)}, f32[288]{0:T(512)}, f32[1152]{0:T(1024)}, f32[288]{0:T(512)}) all-reduce(f32[576]{0:T(1024)S(1)} %dynamic-slice.1, f32[288]{0:T(512)S(1)} %dynamic-slice.3, f32[1152]{0:T(1024)S(1)} %dynamic-slice.5, f32[288]{0:T(512)S(1)} %dynamic-slice.7), channel_id=1, replica_groups=mesh['clip'=8,'frame'=4] {'clip'}, use_global_device_ids=true, to_apply=%region_22.23 | all-reduce | flops 2304 | bytes 18432 | tf_op jit(solution)/shard_map/psum | solution.py:207
  814.9 2.1 copy.81
  816.9 2.5 copy.73
  819.5 2.4 copy.65
  821.9 51.5 %reduce-scatter.34.cloned.1.call-done = f32[576,288]{1,0:T(8,128)} async-done(((f32[4608,288]{1,0:T(8,128)}), f32[576,288]{1,0:T(8,128)}) %reduce-scatter.34.cloned.1.call-update) | async-done | bytes 663568
  873.4 2.3 copy.87
  875.7 33.6 %reduce-scatter.32.cloned.1.call-done = f32[144,288]{1,0:T(8,128)} async-done(((f32[1152,288]{1,0:T(8,128)}), f32[144,288]{1,0:T(8,128)}) %reduce-scatter.32.cloned.1.call-update) | async-done | bytes 165904
  909.3 50.7 %reduce-scatter.30.cloned.1.call-done = f32[144,864]{1,0:T(8,128)} async-done(((f32[1152,864]{1,0:T(8,128)}), f32[144,864]{1,0:T(8,128)}) %reduce-scatter.30.cloned.1.call-update) | async-done | bytes 497680
  960.0 61.6 %reduce-scatter.24.cloned.1.call-done = f32[144,1152]{1,0:T(8,128)} async-done(((f32[1152,1152]{1,0:T(8,128)}), f32[144,1152]{1,0:T(8,128)}) %reduce-scatter.24.cloned.1.call-update) | async-done | bytes 663568 | tf_op jit(solution)/shard_map/reduce_scatter | solution.py:198
  (177 shorter events, 23.8 us)
Async XLA Ops:
  7.2 79.0 %copy-start = (bf16[1152,1152]{1,0:T(8,128)(2,1)S(1)}, bf16[1152,1152]{1,0:T(8,128)(2,1)}, u32[]{:S(2)}) copy-start(bf16[1152,1152]{1,0:T(8,128)(2,1)} %param.17) | copy-start | bytes 7962628
  7.2 8.7 copy-start.37
  7.2 8.8 copy-start.38
  7.2 8.8 copy-start.44
  7.2 8.9 copy-start.42
  10.6 8.9 copy-start.39
  10.6 21.0 %all-to-all-start = ((bf16[2,4,64,1152]{3,1,0,2:T(4,128)(2,1)}), bf16[2,4,64,1152]{3,1,0,2:T(4,128)(2,1)}, u32[]{:S(2)}, u32[]{:S(2)}) async-start(bf16[2,4,64,1152]{3,1,0,2:T(4,128)(2,1)} %copy.57), calls=%async_computation | async-start | bytes 2359296 | tf_op jit(solution)/shard_map/all_to_all | solution.py:53
  16.1 15.5 %copy-start.40 = (f32[2,16]{1,0:T(2,128)}, f32[2,16]{1,0:T(2,128)S(1)}, u32[]{:S(2)}) copy-start(f32[2,16]{1,0:T(2,128)S(1)} %get-tuple-element.97) | copy-start | bytes 388
  19.5 22.2 %copy-start.34 = (f32[2,1152]{1,0:T(2,128)}, f32[2,1152]{1,0:T(2,128)S(1)}, u32[]{:S(2)}) copy-start(f32[2,1152]{1,0:T(2,128)S(1)} %get-tuple-element.106) | copy-start | bytes 27652
  31.6 62.3 %all-to-all-start.2 = ((bf16[2,4,64,1152]{3,1,0,2:T(4,128)(2,1)}), bf16[2,4,64,1152]{3,1,0,2:T(4,128)(2,1)}, u32[]{:S(2)}, u32[]{:S(2)}) async-start(bf16[2,4,64,1152]{3,1,0,2:T(4,128)(2,1)} %copy.66), calls=%async_computation.2 | async-start | bytes 2359296 | tf_op jit(solution)/shard_map/all_to_all | solution.py:116
  35.9 279.5 %reduce-scatter.26.cloned.1.call-start = ((), (), s32[]{:S(2)}) async-start(), calls=%async_computation.17 | async-start | bytes 26542080 | tf_op jit(solution)/shard_map/reduce_scatter | solution.py:188
  37.5 1.4 copy-start.7
  41.7 1.4 copy-start.2
  72.4 2.6 copy-start.15
  72.4 2.6 copy-start.17
  72.4 4.9 copy-start.32
  77.3 1.9 copy-start.27
  86.2 3.3 copy-start.8
  89.5 2.2 copy-start.5
  93.9 2.0 copy-start.3
  95.6 12.9 %copy-start.9 = (f32[2,4,4,16,1152]{4,3,1,2,0:T(8,128)}, f32[2,4,4,16,1152]{4,3,1,2,0:T(8,128)S(1)}, u32[]{:S(2)}) copy-start(f32[2,4,4,16,1152]{4,3,1,2,0:T(8,128)S(1)} %copy.67) | copy-start | bytes 7077892
  98.8 9.5 copy-start.22
  108.4 3.7 copy-start.47
  112.1 1.0 copy-start.33
  123.4 0.7 copy-start.43
  123.5 257.3 %reduce-scatter.20.cloned.1.call-start = ((), (), s32[]{:S(2)}) async-start(), calls=%async_computation.14 | async-start | bytes 6635520 | tf_op jit(solution)/shard_map/reduce_scatter | solution.py:186
  139.9 11.1 %copy-start.21 = (bf16[512,4608]{1,0:T(8,128)(2,1)}, bf16[512,4608]{1,0:T(8,128)(2,1)S(1)}, u32[]{:S(2)}) copy-start(bf16[512,4608]{1,0:T(8,128)(2,1)S(1)} %get-tuple-element.58) | copy-start | bytes 14155780
  139.9 12.5 %copy-start.14 = (f32[2,4,4,16,1152]{4,3,2,1,0:T(8,128)S(1)}, f32[2,4,4,16,1152]{4,3,2,1,0:T(8,128)}, u32[]{:S(2)}) copy-start(f32[2,4,4,16,1152]{4,3,2,1,0:T(8,128)} %get-tuple-element.69) | copy-start | bytes 7077892
  151.0 1.4 copy-start.12
  153.0 4.3 copy-start.10
  157.3 1.6 copy-start.19
  157.9 1.0 copy-start.26
  163.0 368.5 %reduce-scatter.18.cloned.1.call-start = ((), (), s32[]{:S(2)}) async-start(), calls=%async_computation.13 | async-start | bytes 19906560 | tf_op jit(solution)/shard_map/reduce_scatter | solution.py:185
  172.5 7.2 copy-start.30
  172.5 7.2 copy-start.28
  179.7 1.6 copy-start.18
  181.3 1.9 copy-start.16
  183.2 1.7 copy-start.31
  204.3 11.0 %copy-start.4 = (f32[2,4,4,16,1152]{4,3,1,2,0:T(8,128)S(1)}, f32[2,4,4,16,1152]{4,3,1,2,0:T(8,128)}, u32[]{:S(2)}) copy-start(f32[2,4,4,16,1152]{4,3,1,2,0:T(8,128)} %copy-done.2) | copy-start | bytes 7077892
  215.3 9.9 copy-start.36
  215.3 9.9 copy-start.6
  215.3 9.9 copy-start.13
  227.2 13.7 %copy-start.11 = (f32[2,4,4,16,1152]{4,3,1,2,0:T(8,128)S(1)}, f32[2,4,4,16,1152]{4,3,1,2,0:T(8,128)}, u32[]{:S(2)}) copy-start(f32[2,4,4,16,1152]{4,3,1,2,0:T(8,128)} %copy-done.9) | copy-start | bytes 7077892
  227.2 13.7 %copy-start.41 = (f32[2,16]{1,0:T(2,128)S(1)}, f32[2,16]{1,0:T(2,128)}, u32[]{:S(2)}) copy-start(f32[2,16]{1,0:T(2,128)} %copy-done.40) | copy-start | bytes 388
  240.9 2.7 copy-start.35
  243.6 2.2 copy-start.29
  254.2 1.6 copy-start.23
  254.2 470.2 %reduce-scatter.22.cloned.1.call-start = ((), (), s32[]{:S(2)}) async-start(), calls=%async_computation.15 | async-start | bytes 26542080 | tf_op jit(solution)/shard_map/reduce_scatter | solution.py:187
  268.0 546.8 %reduce-scatter.28.cloned.1.call-start = ((), (), s32[]{:S(2)}) async-start(), calls=%async_computation.18 | async-start | bytes 4423680
  271.0 602.4 %reduce-scatter.34.cloned.1.call-start = ((), (), s32[]{:S(2)}) async-start(), calls=%async_computation.21 | async-start | bytes 7962624
  322.1 587.2 %reduce-scatter.32.cloned.1.call-start = ((), (), s32[]{:S(2)}) async-start(), calls=%async_computation.20 | async-start | bytes 1990656
  383.8 576.1 %reduce-scatter.30.cloned.1.call-start = ((), (), s32[]{:S(2)}) async-start(), calls=%async_computation.19 | async-start | bytes 4644864
  537.0 484.5 %reduce-scatter.24.cloned.1.call-start = ((), (), s32[]{:S(2)}) async-start(), calls=%async_computation.16 | async-start | bytes 5971968 | tf_op jit(solution)/shard_map/reduce_scatter | solution.py:198
  724.4 1.3 copy-start.25
  725.6 4.7 copy-start.46
  725.6 7.2 copy-start.45
  725.6 7.5 copy-start.20
  726.8 29.1 %all-to-all-start.3 = ((bf16[2,16,16,1152]{3,2,0,1:T(8,128)(2,1)}), bf16[2,16,16,1152]{3,2,0,1:T(8,128)(2,1)S(1)}, u32[]{:S(2)}, u32[]{:S(2)}) async-start(bf16[2,16,16,1152]{3,2,0,1:T(8,128)(2,1)} %copy.72), calls=%async_computation.3 | async-start | bytes 2359296 | tf_op jit(solution)/shard_map/all_to_all | solution.py:170
  755.9 4.3 copy-start.24
  755.9 63.6 %all-to-all-start.1 = ((bf16[2,16,16,1152]{3,2,0,1:T(8,128)(2,1)}), bf16[2,16,16,1152]{3,2,0,1:T(8,128)(2,1)}, u32[]{:S(2)}, u32[]{:S(2)}) async-start(bf16[2,16,16,1152]{3,2,0,1:T(8,128)(2,1)} %copy.64), calls=%async_computation.1 | async-start | bytes 2359296 | tf_op jit(solution)/shard_map/all_to_all | solution.py:113
  816.9 204.6 %copy-start.1 = (bf16[1152,1152]{1,0:T(8,128)(2,1)S(1)}, bf16[1152,1152]{1,0:T(8,128)(2,1)}, u32[]{:S(2)}) copy-start(bf16[1152,1152]{1,0:T(8,128)(2,1)} %param.17) | copy-start | bytes 7962628
Sparse Core Ops, SparseCore 0:
  123.6 191.7 reduce-scatter.25
  318.7 61.9 reduce-scatter.19
  384.1 147.2 reduce-scatter.17
  534.4 189.9 reduce-scatter.21
  727.6 65.9 reduce-scatter.27
  795.9 77.4 reduce-scatter.33
  876.3 32.9 reduce-scatter.31
  912.3 47.6 reduce-scatter.29
  962.9 58.6 reduce-scatter.23
where the time goes:
time: 1030 us
  waiting for transfers between devices  669 us (65%)
  matrix products  129 us (13%)
  local copies, waits for them, and re-layouts  112 us (11%)
  blocking collectives  52.1 us (5%)
  other arithmetic  31.5 us (3%)
  starting transfers between devices  17.8 us (2%)
  between operations  16.9 us (2%)
    reduce_scatter x1, waiting for transfers between devices, on_device(): lax.psum_scatter(d_fc1_weight, 'frame', scatter_dimension=1, tiled=True)  187 us
    reduce_scatter x1, waiting for transfers between devices, on_device(): lax.psum_scatter(d_qkv_weight, 'frame', scatter_dimension=1, tiled=True)  148 us
    unnamed x13, waiting for transfers between devices  136 us
    reduce_scatter x1, waiting for transfers between devices, on_device(): lax.psum_scatter(every_part[2], 'clip', scatter_dimension=0, tiled=True)  61.6 us
    reduce_scatter x1, waiting for transfers between devices, on_device(): lax.psum_scatter(d_out_weight, 'frame', scatter_dimension=1, tiled=True)  58.5 us
    reduce_scatter x1, waiting for transfers between devices, on_device(): lax.psum_scatter(d_fc2_weight, 'frame', scatter_dimension=1, tiled=True)  44.4 us
    unnamed x113, local copies, waits for them, and re-layouts  43.8 us
    dot_general x4, matrix products, contract_cols(): lax.dot_general(left, right, (((1,), (1,)), ((), ())), preferred_element_...  40.8 us
  transfers between devices with their start and end apart: 13, of which 10 were waited for; matrix products, arithmetic and copies ran while one was open for 22% of the time, Pallas kernels for 0%

commit v1 on v0

--- a/solution.py
+++ b/solution.py
@@ -1,6 +1,8 @@
 import jax
 import jax.numpy as jnp
 from jax import lax
+from jax.experimental import pallas as pl
+from jax.experimental.pallas import tpu as pltpu
 from jax.sharding import PartitionSpec as P
 
 HEADS = 16
@@ -220,6 +222,971 @@
     )
 
 
+LANES = 128
+VMEM_LIMIT = 58 * 1024 * 1024
+ROWS_DN = (((0,), (0,)), ((), ()))
+COLS_DN = (((1,), (1,)), ((), ()))
+F32 = jnp.float32
+BF16 = jnp.bfloat16
+
+
+def mm(left, right):
+    return jnp.dot(left, right, preferred_element_type=F32)
+
+
+def mm_cols(left, right):
+    return lax.dot_general(left, right, COLS_DN, preferred_element_type=F32)
+
+
+def mm_rows(left, right):
+    return lax.dot_general(left, right, ROWS_DN, preferred_element_type=F32)
+
+
+def unit(values):
+    centred = values - jnp.mean(values, axis=-1, keepdims=True)
+    variance = jnp.mean(centred * centred, axis=-1, keepdims=True)
+    inverse = lax.rsqrt(variance + EPSILON)
+    return centred * inverse, inverse
+
+
+def unit_back(unit_values, inverse, grad):
+    mean_grad = jnp.mean(grad, axis=-1, keepdims=True)
+    mean_dot = jnp.mean(grad * unit_values, axis=-1, keepdims=True)
+    return (grad - mean_grad - unit_values * mean_dot) * inverse
+
+
+def params(**more):
+    return pltpu.CompilerParams(vmem_limit_bytes=VMEM_LIMIT, **more)
+
+
+def cost(flops, moved, transcendentals=0):
+    return pl.CostEstimate(flops=int(flops), bytes_accessed=int(moved), transcendentals=int(transcendentals))
+
+
+def shape(dims, kind):
+    return jax.ShapeDtypeStruct(tuple(dims), kind)
+
+
+def whole(dims, buffers=1):
+    zeros = (0,) * len(dims)
+    return pl.BlockSpec(tuple(dims), lambda *_: zeros, pipeline_mode=pl.Buffered(buffers))
+
+
+ANY = pl.BlockSpec(memory_space=pl.ANY)
+
+
+def head_window(head, width):
+    low = head * width
+    start = low // LANES * LANES
+    size = LANES if low - start + width <= LANES else 2 * LANES
+    return low, start, size
+
+
+def head_mask(head, width):
+    low, start, size = head_window(head, width)
+    lane = lax.broadcasted_iota(jnp.int32, (1, size), 1) + start
+    return jnp.where((lane >= low) & (lane < low + width), 1.0, 0.0).astype(BF16)
+
+
+class Plan:
+    def __init__(self, mesh, x, qkv_weight, fc1_weight):
+        self.clip_axis = mesh.shape["clip"]
+        self.frame_axis = mesh.shape["frame"]
+        self.clips, self.local_frames, self.patches, self.width = x
+        self.own_patches = self.patches // self.frame_axis
+        self.halves = self.own_patches // 8
+        self.frames = self.local_frames * self.frame_axis
+        self.ff = fc1_weight[1]
+        self.rows = self.clips * self.frames * self.own_patches
+        self.clip_rows = self.rows // self.clips
+        self.block = self.frames * 8
+        self.blocks = self.rows // self.block
+        self.piece = self.local_frames * 8
+        self.head_width = self.width // HEADS
+        self.chunk_dims = (self.clips, self.halves, self.local_frames, 8, self.width)
+        self.zs = self.clip_axis // 2
+
+    def row_of(self, clip, half, k):
+        return ((clip * self.halves + half) * self.frame_axis + k) * self.piece
+
+
+def fits(mesh, x, qkv_weight, fc1_weight):
+    clip_axis, frame_axis = mesh.shape["clip"], mesh.shape["frame"]
+    width, ff = x[3], fc1_weight[1]
+    return (
+        clip_axis == 8
+        and frame_axis == 4
+        and x[2] // frame_axis % 8 == 0
+        and x[1] * frame_axis * 8 == LANES
+        and width == 1152
+        and ff == 4 * width
+        and qkv_weight[1] == 3 * width
+    )
+
+
+def split_chunks(plan, me, x):
+    n, own = plan.frame_axis, plan.own_patches
+
+    def body(me_ref, *refs):
+        for k in range(n):
+            for half in range(plan.halves):
+                refs[n + k][0, half] = refs[k][0, :, half * 8 : half * 8 + 8, :]
+
+    def source(k):
+        return pl.BlockSpec(
+            (1, plan.local_frames, own, plan.width),
+            lambda c, me_ref: (c, 0, jnp.bitwise_xor(me_ref[0], k), 0),
+        )
+
+    return pl.pallas_call(
+        body,
+        grid_spec=pltpu.PrefetchScalarGridSpec(
+            num_scalar_prefetch=1,
+            grid=(plan.clips,),
+            in_specs=[source(k) for k in range(n)],
+            out_specs=[pl.BlockSpec((1,) + plan.chunk_dims[1:], lambda c, me_ref: (c, 0, 0, 0, 0))] * n,
+        ),
+        out_shape=[shape(plan.chunk_dims, BF16)] * n,
+        compiler_params=params(),
+        cost_estimate=cost(0, 4 * plan.rows * plan.width),
+        name="split_chunks",
+    )(me, *([x] * n))
+
+
+def join_chunks(plan, me, chunks):
+    n, own = plan.frame_axis, plan.own_patches
+
+    def body(me_ref, *refs):
+        out = refs[n]
+        for k in range(n):
+            place = jnp.bitwise_xor(me_ref[0], k) * own
+            for half in range(plan.halves):
+                out[0, :, pl.ds(pl.multiple_of(place + half * 8, 8), 8), :] = refs[k][0, half]
+
+    return pl.pallas_call(
+        body,
+        grid_spec=pltpu.PrefetchScalarGridSpec(
+            num_scalar_prefetch=1,
+            grid=(plan.clips,),
+            in_specs=[pl.BlockSpec((1,) + plan.chunk_dims[1:], lambda c, me_ref: (c, 0, 0, 0, 0))] * n,
+            out_specs=pl.BlockSpec((1, plan.local_frames, plan.patches, plan.width), lambda c, me_ref: (c, 0, 0, 0)),
+        ),
+        out_shape=shape((plan.clips, plan.local_frames, plan.patches, plan.width), BF16),
+        compiler_params=params(),
+        cost_estimate=cost(0, 4 * plan.rows * plan.width),
+        name="join_chunks",
+    )(me, *chunks)
+
+
+def exchange(plan, chunks):
+    n = plan.frame_axis
+    return [chunks[0]] + [
+        lax.ppermute(chunks[k], "frame", [(i, i ^ k) for i in range(n)]) for k in range(1, n)
+    ]
+
+
+def forward(plan, chunks, mods, score_mask, qkv_weight, bias_full, out_weight, out_bias, fc1_weight, fc1_bias):
+    n, rows, width, ff = plan.frame_axis, plan.rows, plan.width, plan.ff
+    fblocks = ff // width
+    first_attn, after_attn = 3, 3 + plan.blocks
+    steps = after_attn + 1 + fblocks
+    block = plan.block
+
+    def body(*refs):
+        xs = refs[:n]
+        (mod, mask, wqkv, bqkv, wout, bout, w1, b1, probs, gp, act) = refs[n : n + 11]
+        outs = refs[n + 11 : n + 18]
+        x_s, n1_s, proj_s, ctx_s, att_s, mid_s, n2_s, acc_s, sems = refs[n + 18 :]
+        stores = (x_s, n1_s, proj_s, ctx_s, att_s, mid_s, n2_s)
+        step = pl.program_id(0)
+
+        def push(i):
+            pltpu.make_async_copy(stores[i], outs[i], sems.at[i]).start()
+
+        @pl.when(step == 0)
+        def _():
+            for c in range(plan.clips):
+                shift, scale = mod[c, 0:1, :], 1.0 + mod[c, 1:2, :]
+                for half in range(plan.halves):
+                    for k in range(n):
+                        row = plan.row_of(c, half, k)
+                        piece = xs[k][c, half].astype(F32).reshape(plan.piece, width)
+                        x_s[row : row + plan.piece, :] = piece
+                        normed, _ = unit(piece)
+                        n1_s[row : row + plan.piece, :] = (normed * scale + shift).astype(BF16)
+            push(0)
+            push(1)
+
+        @pl.when(step < first_attn)
+        def _():
+            proj_s[step] = (mm(n1_s[...], wqkv[...]) + bqkv[...]).astype(BF16)
+
+        @pl.when(step == first_attn)
+        def _():
+            push(2)
+
+        @pl.when((step >= first_attn) & (step < after_attn))
+        def _():
+            at = step - first_attn
+            here = pl.ds(pl.multiple_of(at * block, block), block)
+            allowed = mask[at // plan.halves]
+            acc_s[...] = jnp.zeros_like(acc_s)
+            for h in range(HEADS):
+                _, start, size = head_window(h, plan.head_width)
+                keep = head_mask(h, plan.head_width)
+                cols = slice(start, start + size)
+                q = proj_s[0, here, cols] * keep
+                v = proj_s[2, here, cols] * keep
+                score = mm_cols(q, proj_s[1, here, cols]) * (plan.head_width ** (-0.5)) + allowed
+                grown = jnp.exp(score - jnp.max(score, axis=-1, keepdims=True))
+                weight = grown * (1.0 / jnp.sum(grown, axis=-1, keepdims=True))
+                probs[0, h] = weight
+                acc_s[:, cols] += mm(weight.astype(BF16), v)
+            ctx_s[here, :] = acc_s[...].astype(BF16)
+
+        @pl.when(step == after_attn)
+        def _():
+            push(3)
+            att_s[...] = mm(ctx_s[...], wout[...]) + bout[...]
+            push(4)
+            for c in range(plan.clips):
+                here = slice(c * plan.clip_rows, (c + 1) * plan.clip_rows)
+                middle = x_s[here, :] + mod[c, 2:3, :] * att_s[here, :]
+                mid_s[here, :] = middle
+                normed, _ = unit(middle)
+                n2_s[here, :] = (normed * (1.0 + mod[c, 4:5, :]) + mod[c, 3:4, :]).astype(BF16)
+            push(5)
+            push(6)
+
+        @pl.when(step > after_attn)
+        def _():
+            hidden = mm(n2_s[...], w1[...]) + b1[...]
+            square = hidden * hidden
+            inner = 0.7978845608028654 * hidden * (1.0 + 0.044715 * square)
+            bent = jnp.tanh(inner)
+            act[...] = (0.5 * hidden * (1.0 + bent)).astype(BF16)
+            slope = 0.7978845608028654 * (1.0 + 3.0 * 0.044715 * square)
+            gp[...] = 0.5 * (1.0 + bent) + 0.5 * hidden * (1.0 - bent * bent) * slope
+
+        @pl.when(step == steps - 1)
+        def _():
+            for i in range(len(stores)):
+                pltpu.make_async_copy(stores[i], outs[i], sems.at[i]).wait()
+
+    ff_at = lambda i: (0, jnp.clip(i - after_attn - 1, 0, fblocks - 1))
+    saved = [
+        shape((rows, width), F32),
+        shape((rows, width), BF16),
+        shape((3, rows, width), BF16),
+        shape((rows, width), BF16),
+        shape((rows, width), F32),
+        shape((rows, width), F32),
+        shape((rows, width), BF16),
+    ]
+    result = pl.pallas_call(
+        body,
+        grid=(steps,),
+        in_specs=[whole(plan.chunk_dims)] * n
+        + [
+            whole((plan.clips, 6, width)),
+            whole((plan.clips, block, block)),
+            pl.BlockSpec((width, width), lambda i: (0, jnp.minimum(i, 2))),
+            pl.BlockSpec((1, width), lambda i: (0, jnp.minimum(i, 2))),
+            whole((width, width)),
+            whole((1, width)),
+            pl.BlockSpec((width, width), ff_at),
+            pl.BlockSpec((1, width), ff_at),
+        ],
+        out_specs=[
+            pl.BlockSpec(
+                (1, HEADS, block, block),
+                lambda i: (jnp.clip(i - first_attn, 0, plan.blocks - 1), 0, 0, 0),
+            ),
+            pl.BlockSpec((rows, width), ff_at),
+            pl.BlockSpec((rows, width), ff_at),
+        ]
+        + [ANY] * len(saved),
+        out_shape=[
+            shape((plan.blocks, HEADS, block, block), F32),
+            shape((rows, ff), F32),
+            shape((rows, ff), BF16),
+        ]
+        + saved,
+        scratch_shapes=[pltpu.VMEM(s.shape, s.dtype) for s in saved]
+        + [pltpu.VMEM((block, width), F32), pltpu.SemaphoreType.DMA((len(saved),))],
+        compiler_params=params(),
+        cost_estimate=cost(18e9, 60e6, 4e6),
+        name="forward",
+    )(*chunks, mods, score_mask, qkv_weight, bias_full, out_weight, out_bias, fc1_weight, fc1_bias)
+    names = ("probs", "gp", "act", "x", "n1", "proj", "ctx", "att", "mid", "n2")
+    return dict(zip(names, result))
+
+
+def put_slabs(ref, z, f, at, values, tiles):
+    rows = values.shape[0]
+    for j in range(tiles):
+        ref[z, f, at + j * rows : at + (j + 1) * rows, :] = values[:, j * LANES : (j + 1) * LANES].astype(BF16)
+
+
+def fold_tile(tile, folds, used):
+    rows = tile.shape[0] // folds
+    total = tile[:rows]
+    for g in range(1, folds):
+        total = total + pltpu.roll(tile[g * rows : (g + 1) * rows], g * used, 1)
+    return total
+
+
+def fc2_grad(plan, core, cot_chunks, mods, row_valid, act):
+    n, rows, width = plan.frame_axis, plan.rows, plan.width
+    span = plan.ff // plan.clip_axis
+    wide = width // n
+    padded = -(-wide // LANES) * LANES
+    tail = wide % LANES
+    folds = LANES // tail
+    slab_rows = wide // LANES * span + span // folds
+
+    def body(core_ref, *refs):
+        cots = refs[:n]
+        mod, valid, a, send, keep, dbr, dres, bias, padded_s, res_s, bias_s = refs[n:]
+        step = pl.program_id(0)
+
+        @pl.when(step == 0)
+        def _():
+            padded_s[...] = jnp.zeros_like(padded_s)
+            total = jnp.zeros((1, width), F32)
+            for c in range(plan.clips):
+                for half in range(plan.halves):
+                    for k in range(n):
+                        row = plan.row_of(c, half, k)
+                        here = slice(row, row + plan.piece)
+                        piece = cots[k][c, half].astype(F32).reshape(plan.piece, width)
+                        piece = piece * valid[here, 0:1]
+                        dres[here, :] = piece.astype(BF16)
+                        low = (piece * mod[c, 5:6, :]).astype(BF16)
+                        dbr[here, :] = low
+                        total = total + jnp.sum(low.astype(F32), axis=0, keepdims=True)
+            bias[...] = total
+            for f in range(n):
+                padded_s[:, f * padded : f * padded + wide] = dbr[:, f * wide : (f + 1) * wide]
+
+        res_s[...] = mm_rows(a[...], padded_s[...])
+        for ref, part in ((send, 1 - core_ref[0]), (keep, core_ref[0])):
+            at = pl.ds(pl.multiple_of(part * span, 8), span)
+            for f in range(n):
+                main = padded - LANES
+                for j in range(main // LANES):
+                    lanes = slice(f * padded + j * LANES, f * padded + (j + 1) * LANES)
+                    ref[0, f, j * span : (j + 1) * span, :] = res_s[at, lanes].astype(BF16)
+                lanes = slice(f * padded + main, (f + 1) * padded)
+                ref[0, f, main // LANES * span :, :] = fold_tile(res_s[at, lanes], folds, tail).astype(BF16)
+
+    slab = (1, n, slab_rows, LANES)
+    return pl.pallas_call(
+        body,
+        grid_spec=pltpu.PrefetchScalarGridSpec(
+            num_scalar_prefetch=1,
+            grid=(plan.zs,),
+            in_specs=[whole(plan.chunk_dims)] * n
+            + [
+                whole((plan.clips, 6, width)),
+                whole((rows, LANES)),
+                pl.BlockSpec((rows, 2 * span), lambda i, core_ref: (0, i)),
+            ],
+            out_specs=[pl.BlockSpec(slab, lambda i, core_ref: (i, 0, 0, 0))] * 2
+            + [whole((rows, width)), whole((rows, width)), whole((1, width))],
+            scratch_shapes=[
+                pltpu.VMEM((rows, n * padded), BF16),
+                pltpu.VMEM((2 * span, n * padded), F32),
+                pltpu.VMEM((1, width), F32),
+            ],
+        ),
+        out_shape=[shape((plan.zs, n, slab_rows, LANES), BF16)] * 2
+        + [shape((rows, width), BF16), shape((rows, width), BF16), shape((1, width), F32)],
+        compiler_params=params(),
+        cost_estimate=cost(7e9, 20e6),
+        name="fc2_grad",
+    )(core, *cot_chunks, mods, row_valid, act)
+
+
+def hidden_grad(plan, d_branch, fc2_weight, gp):
+    rows, width, ff = plan.rows, plan.width, plan.ff
+
+    def body(dbr, w2, slope, dh, bias):
+        low = (mm_cols(dbr[...], w2[...]) * slope[...]).astype(BF16)
+        dh[...] = low
+        bias[...] = jnp.sum(low.astype(F32), axis=0, keepdims=True)
+
+    return pl.pallas_call(
+        body,
+        grid=(ff // width,),
+        in_specs=[
+            whole((rows, width)),
+            pl.BlockSpec((width, width), lambda i: (i, 0)),
+            pl.BlockSpec((rows, width), lambda i: (0, i)),
+        ],
+        out_specs=[pl.BlockSpec((rows, width), lambda i: (0, i)), pl.BlockSpec((1, width), lambda i: (0, i))],
+        out_shape=[shape((rows, ff), BF16), shape((1, ff), F32)],
+        compiler_params=params(),
+        cost_estimate=cost(5.4e9, 26e6),
+        name="hidden_grad",
+    )(d_branch, fc2_weight, gp)
+
+
+def fc1_grad(plan, core, n2, d_hidden):
+    n, rows, width, ff = plan.frame_axis, plan.rows, plan.width, plan.ff
+    span = width // plan.clip_axis
+    wide = ff // n
+    slab_rows = wide // LANES * span
+
+    def body(core_ref, left, dh, send, keep, turned_s, res_s):
+        @pl.when(pl.program_id(0) == 0)
+        def _():
+            turned_s[...] = left[...].T
+
+        res_s[...] = mm(turned_s[...], dh[...])
+        for ref, part in ((send, 1 - core_ref[0]), (keep, core_ref[0])):
+            for z in range(plan.zs):
+                at = pl.ds(pl.multiple_of((2 * z + part) * span, 8), span)
+                for j in range(wide // LANES):
+                    ref[z, 0, j * span : (j + 1) * span, :] = res_s[at, j * LANES : (j + 1) * LANES].astype(BF16)
+
+    slab = (plan.zs, 1, slab_rows, LANES)
+    return pl.pallas_call(
+        body,
+        grid_spec=pltpu.PrefetchScalarGridSpec(
+            num_scalar_prefetch=1,
+            grid=(n,),
+            in_specs=[whole((rows, width)), pl.BlockSpec((rows, wide), lambda i, core_ref: (0, i))],
+            out_specs=[pl.BlockSpec(slab, lambda i, core_ref: (0, i, 0, 0))] * 2,
+            scratch_shapes=[pltpu.VMEM((width, rows), BF16), pltpu.VMEM((width, wide), F32)],
+        ),
+        out_shape=[shape((plan.zs, n, slab_rows, LANES), BF16)] * 2,
+        compiler_params=params(),
+        cost_estimate=cost(5.4e9, 17e6),
+        name="fc1_grad",
+    )(core, n2, d_hidden)
+
+
+def middle_grad(plan, d_hidden, fc1_weight, mods, mid, att, d_result, out_weight):
+    rows, width, ff = plan.rows, plan.width, plan.ff
+    steps = ff // width
+
+    def body(dh, w1, mod, mid_r, att_r, dres, wout, dmid, datt, dctx, dmod, bias, acc):
+        step = pl.program_id(0)
+
+        @pl.when(step == 0)
+        def _():
+            acc[...] = mm_cols(dh[...], w1[...])
+
+        @pl.when(step > 0)
+        def _():
+            acc[...] += mm_cols(dh[...], w1[...])
+
+        @pl.when(step == steps - 1)
+        def _():
+            total = jnp.zeros((1, width), F32)
+            for c in range(plan.clips):
+                here = slice(c * plan.clip_rows, (c + 1) * plan.clip_rows)
+                normed, inverse = unit(mid_r[here, :])
+                grad = acc[here, :]
+                dmod[c, 1:2, :] = jnp.sum(grad, axis=0, keepdims=True)
+                dmod[c, 2:3, :] = jnp.sum(grad * normed, axis=0, keepdims=True)
+                d_middle = dres[here, :].astype(F32) + unit_back(normed, inverse, grad * (1.0 + mod[c, 4:5, :]))
+                dmid[here, :] = d_middle
+                dmod[c, 0:1, :] = jnp.sum(d_middle * att_r[here, :], axis=0, keepdims=True)
+                low = (d_middle * mod[c, 2:3, :]).astype(BF16)
+                datt[here, :] = low
+                total = total + jnp.sum(low.astype(F32), axis=0, keepdims=True)
+            bias[...] = total
+            dctx[...] = mm_cols(datt[...], wout[...]).astype(BF16)
+
+    return pl.pallas_call(
+        body,
+        grid=(steps,),
+        in_specs=[
+            pl.BlockSpec((rows, width), lambda i: (0, i)),
+            pl.BlockSpec((width, width), lambda i: (0, i)),
+            whole((plan.clips, 6, width)),
+            whole((rows, width)),
+            whole((rows, width)),
+            whole((rows, width)),
+            whole((width, width)),
+        ],
+        out_specs=[
+            whole((rows, width)),
+            whole((rows, width)),
+            whole((rows, width)),
+            whole((plan.clips, 3, width)),
+            whole((1, width)),
+        ],
+        out_shape=[
+            shape((rows, width), F32),
+            shape((rows, width), BF16),
+            shape((rows, width), BF16),
+            shape((plan.clips, 3, width), F32),
+            shape((1, width), F32),
+        ],
+        scratch_shapes=[pltpu.VMEM((rows, width), F32)],
+        compiler_params=params(),
+        cost_estimate=cost(7e9, 30e6),
+        name="middle_grad",
+    )(d_hidden, fc1_weight, mods, mid, att, d_result, out_weight)
+
+
+def attention_grad(plan, proj, probs, d_context):
+    rows, width, block = plan.rows, plan.width, plan.block
+    factor = plan.head_width ** (-0.5)
+
+    def body(p, w, dctx, dproj, sums, acc):
+        acc[...] = jnp.zeros_like(acc)
+        for h in range(HEADS):
+            _, start, size = head_window(h, plan.head_width)
+            keep = head_mask(h, plan.head_width)
+            cols = slice(start, start + size)
+            weight = w[0, h]
+            low = weight.astype(BF16)
+            d_c = dctx[:, cols] * keep
+            d_weight = mm_cols(d_c, p[2, :, cols])
+            mixed = weight * d_weight
+            d_score = (mixed - weight * jnp.sum(mixed, axis=-1, keepdims=True)).astype(BF16)
+            acc[2, :, cols] += mm_rows(low, d_c)
+            acc[0, :, cols] += mm(d_score, p[1, :, cols] * keep)
+            acc[1, :, cols] += mm_rows(d_score, p[0, :, cols] * keep)
+        for part in range(3):
+            values = acc[part] if part == 2 else acc[part] * factor
+            low = values.astype(BF16)
+            dproj[part] = low
+            sums[0, part : part + 1, :] = jnp.sum(low.astype(F32), axis=0, keepdims=True)
+
+    return pl.pallas_call(
+        body,
+        grid=(plan.blocks,),
+        in_specs=[
+            pl.BlockSpec((3, block, width), lambda i: (0, i, 0)),
+            pl.BlockSpec((1, HEADS, block, block), lambda i: (i, 0, 0, 0)),
+            pl.BlockSpec((block, width), lambda i: (i, 0)),
+        ],
+        out_specs=[
+            pl.BlockSpec((3, block, width), lambda i: (0, i, 0)),
+            pl.BlockSpec((1, 3, width), lambda i: (i, 0, 0)),
+        ],
+        out_shape=[shape((3, rows, width), BF16), shape((plan.blocks, 3, width), F32)],
+        scratch_shapes=[pltpu.VMEM((3, block, width), F32)],
+        compiler_params=params(),
+        cost_estimate=cost(4e9, 14e6),
+        name="attention_grad",
+    )(proj, probs, d_context)
+
+
+def attention_weight_grads(plan, core, n1, ctx, d_proj, d_att):
+    n, rows, width = plan.frame_axis, plan.rows, plan.width
+    span = width // plan.clip_axis
+    wide = 3 * width // n
+    padded = -(-wide // LANES) * LANES
+    out_wide = width // n
+    out_padded = -(-out_wide // LANES) * LANES
+    out_tail = out_wide % LANES
+    folds = 3
+    first_rows = padded // LANES * span
+    slab_rows = first_rows + out_wide // LANES * span + span // folds
+
+    def body(core_ref, left_q, left_o, dp, da, send, keep, turn_q, turn_o, right_q, right_o, res_q, res_o):
+        f_now = pl.program_id(0)
+
+        @pl.when(f_now == 0)
+        def _():
+            turn_q[...] = left_q[...].T
+            turn_o[...] = left_o[...].T
+            right_q[...] = jnp.zeros_like(right_q)
+            right_o[...] = jnp.zeros_like(right_o)
+            for f in range(n):
+                right_o[f, :, :out_wide] = da[:, f * out_wide : (f + 1) * out_wide]
+                low, high = f * wide, (f + 1) * wide
+                for part in range(3):
+                    a, b = max(low, part * width), min(high, (part + 1) * width)
+                    if a < b:
+                        right_q[f, :, a - low : b - low] = dp[part, :, a - part * width : b - part * width]
+
+        res_q[...] = mm(turn_q[...], right_q[f_now])
+        res_o[...] = mm(turn_o[...], right_o[f_now])
+        for ref, part in ((send, 1 - core_ref[0]), (keep, core_ref[0])):
+            for z in range(plan.zs):
+                at = pl.ds(pl.multiple_of((2 * z + part) * span, 8), span)
+                for j in range(padded // LANES):
+                    ref[z, 0, j * span : (j + 1) * span, :] = res_q[at, j * LANES : (j + 1) * LANES].astype(BF16)
+                for j in range(out_wide // LANES):
+                    row = first_rows + j * span
+                    ref[z, 0, row : row + span, :] = res_o[at, j * LANES : (j + 1) * LANES].astype(BF16)
+                row = first_rows + out_wide // LANES * span
+                tile = fold_tile(res_o[at, out_padded - LANES : out_padded], folds, out_tail)
+                ref[z, 0, row : row + span // folds, :] = tile.astype(BF16)
+
+    slab = (plan.zs, 1, slab_rows, LANES)
+    return pl.pallas_call(
+        body,
+        grid_spec=pltpu.PrefetchScalarGridSpec(
+            num_scalar_prefetch=1,
+            grid=(n,),
+            in_specs=[
+                whole((rows, width)),
+                whole((rows, width)),
+                whole((3, rows, width)),
+                whole((rows, width)),
+            ],
+            out_specs=[pl.BlockSpec(slab, lambda i, core_ref: (0, i, 0, 0))] * 2,
+            scratch_shapes=[
+                pltpu.VMEM((width, rows), BF16),
+                pltpu.VMEM((width, rows), BF16),
+                pltpu.VMEM((n, rows, padded), BF16),
+                pltpu.VMEM((n, rows, out_padded), BF16),
+                pltpu.VMEM((width, padded), F32),
+                pltpu.VMEM((width, out_padded), F32),
+            ],
+        ),
+        out_shape=[shape((plan.zs, n, slab_rows, LANES), BF16)] * 2,
+        compiler_params=params(),
+        cost_estimate=cost(6e9, 18e6),
+        name="attention_weight_grads",
+    )(core, n1, ctx, d_proj, d_att)
+
+
+def input_grad_rows(plan, d_proj, qkv_weight, mods, x, d_middle):
+    n, rows, width = plan.frame_axis, plan.rows, plan.width
+
+    def body(dp, w, mod, x_r, dmid, *refs):
+        outs, dmod, acc = refs[:n], refs[n], refs[n + 1]
+        step = pl.program_id(0)
+
+        @pl.when(step == 0)
+        def _():
+            acc[...] = mm_cols(dp[0], w[...])
+
+        @pl.when(step > 0)
+        def _():
+            acc[...] += mm_cols(dp[0], w[...])
+
+        @pl.when(step == 2)
+        def _():
+            for c in range(plan.clips):
+                here = slice(c * plan.clip_rows, (c + 1) * plan.clip_rows)
+                normed, inverse = unit(x_r[here, :])
+                grad = acc[here, :]
+                dmod[c, 0:1, :] = jnp.sum(grad, axis=0, keepdims=True)
+                dmod[c, 1:2, :] = jnp.sum(grad * normed, axis=0, keepdims=True)
+                total = dmid[here, :] + unit_back(normed, inverse, grad * (1.0 + mod[c, 1:2, :]))
+                for half in range(plan.halves):
+                    for k in range(n):
+                        row = plan.row_of(0, half, k)
+                        piece = total[row : row + plan.piece, :].reshape(plan.local_frames, 8, width)
+                        outs[k][c, half] = piece.astype(BF16)
+
+    return pl.pallas_call(
+        body,
+        grid=(3,),
+        in_specs=[
+            pl.BlockSpec((1, rows, width), lambda i: (i, 0, 0)),
+            pl.BlockSpec((width, width), lambda i: (0, i)),
+            whole((plan.clips, 6, width)),
+            whole((rows, width)),
+            whole((rows, width)),
+        ],
+        out_specs=[whole(plan.chunk_dims)] * n + [whole((plan.clips, 2, width))],
+        out_shape=[shape(plan.chunk_dims, BF16)] * n + [shape((plan.clips, 2, width), F32)],
+        scratch_shapes=[pltpu.VMEM((rows, width), F32)],
+        compiler_params=params(),
+        cost_estimate=cost(4e9, 20e6),
+        name="input_grad_rows",
+    )(d_proj, qkv_weight, mods, x, d_middle)
+
+
+def output_rows(plan, act, fc2_weight, fc2_bias, mods, mid, d_result, row_valid):
+    n, rows, width, ff = plan.frame_axis, plan.rows, plan.width, plan.ff
+    steps = ff // width
+
+    def body(a, w, bias, mod, mid_r, dres, valid, *refs):
+        outs, dmod, acc = refs[:n], refs[n], refs[n + 1]
+        step = pl.program_id(0)
+
+        @pl.when(step == 0)
+        def _():
+            acc[...] = mm(a[...], w[...])
+
+        @pl.when(step > 0)
+        def _():
+            acc[...] += mm(a[...], w[...])
+
+        @pl.when(step == steps - 1)
+        def _():
+            for c in range(plan.clips):
+                here = slice(c * plan.clip_rows, (c + 1) * plan.clip_rows)
+                branch = acc[here, :] + bias[...]
+                dmod[c, 0:1, :] = jnp.sum(dres[here, :].astype(F32) * branch, axis=0, keepdims=True)
+                total = valid[here, 0:1] * (mid_r[here, :] + mod[c, 5:6, :] * branch)
+                for half in range(plan.halves):
+                    for k in range(n):
+                        row = plan.row_of(0, half, k)
+                        piece = total[row : row + plan.piece, :].reshape(plan.local_frames, 8, width)
+                        outs[k][c, half] = piece.astype(BF16)
+
+    return pl.pallas_call(
+        body,
+        grid=(steps,),
+        in_specs=[
+            pl.BlockSpec((rows, width), lambda i: (0, i)),
+            pl.BlockSpec((width, width), lambda i: (i, 0)),
+            whole((1, width)),
+            whole((plan.clips, 6, width)),
+            whole((rows, width)),
+            whole((rows, width)),
+            whole((rows, LANES)),
+        ],
+        out_specs=[whole(plan.chunk_dims)] * n + [whole((plan.clips, 1, width))],
+        out_shape=[shape(plan.chunk_dims, BF16)] * n + [shape((plan.clips, 1, width), F32)],
+        scratch_shapes=[pltpu.VMEM((rows, width), F32)],
+        compiler_params=params(),
+        cost_estimate=cost(5.4e9, 26e6),
+        name="output_rows",
+    )(act, fc2_weight, fc2_bias, mods, mid, d_result, row_valid)
+
+
+BIT_OF = {"core": ("clip", 1), "z0": ("clip", 2), "z1": ("clip", 4), "x": ("frame", 1), "y": ("frame", 2)}
+BIT_AT = ("core", "x", "y", "z0", "z1")
+ORDERS = (("x", "z0", "z1", "y"), ("y", "z0", "z1", "x"))
+
+
+def swap(plan, value, bit):
+    axis, step = BIT_OF[bit]
+    size = plan.clip_axis if axis == "clip" else plan.frame_axis
+    return lax.ppermute(value, axis, [(i, i ^ step) for i in range(size)])
+
+
+def add_split(bits, parts):
+    count = 2 ** (len(parts[0][5]) - 1)
+
+    def body(bits_ref, *refs):
+        m = len(parts)
+        for i in range(m):
+            a_send, a_keep, b_send, b_keep = refs[4 * i : 4 * i + 4]
+            send, keep = refs[4 * m + 2 * i : 4 * m + 2 * i + 2]
+            send[...] = (a_send[...].astype(F32) + b_send[...].astype(F32)).astype(BF16)
+            keep[...] = (a_keep[...].astype(F32) + b_keep[...].astype(F32)).astype(BF16)
+
+    in_specs, operands, out_specs, out_shape = [], [], [], []
+    moved = 0
+    for kept, kept_at, received, received_at, rows, left, bit in parts:
+        place = len(left) - 1 - left.index(bit)
+        which = BIT_AT.index(bit)
+
+        def at(row_block, mine, place=place, which=which):
+            def index(i, bits_ref):
+                value = bits_ref[which] if mine else 1 - bits_ref[which]
+                low = i % (2**place)
+                return ((i // (2**place)) * (2 ** (place + 1)) + value * (2**place) + low, row_block, 0)
+
+            return index
+
+        for array, row_block in ((kept, kept_at), (received, received_at)):
+            for mine in (False, True):
+                in_specs.append(pl.BlockSpec((1, rows, LANES), at(row_block, mine)))
+                operands.append(array)
+        out_specs += [pl.BlockSpec((1, rows, LANES), lambda i, bits_ref: (i, 0, 0))] * 2
+        out_shape += [shape((count, rows, LANES), BF16)] * 2
+        moved += 6 * count * rows * LANES * 2
+    result = pl.pallas_call(
+        body,
+        grid_spec=pltpu.PrefetchScalarGridSpec(
+            num_scalar_prefetch=1, grid=(count,), in_specs=in_specs, out_specs=out_specs
+        ),
+        out_shape=out_shape,
+        compiler_params=params(),
+        cost_estimate=cost(moved // 4, moved),
+        name="add_split",
+    )(bits, *operands)
+    return [(result[2 * i], result[2 * i + 1]) for i in range(len(parts))]
+
+
+class Scatter:
+    def __init__(self, plan, bits, send, keep, orders):
+        zs, n, rows, lanes = send.shape
+        self.plan, self.bits, self.orders = plan, bits, orders
+        self.rows = rows // len(orders)
+        received = swap(plan, send.reshape(zs * n, rows, lanes), "core")
+        keep = keep.reshape(zs * n, rows, lanes)
+        self.state = [(keep, t, received, t) for t in range(len(orders))]
+        self.left = [("z1", "z0", "y", "x")] * len(orders)
+        self.stage = 0
+
+    def advance(self):
+        parts = [
+            state + (self.rows, left, order[self.stage])
+            for state, left, order in zip(self.state, self.left, self.orders)
+        ]
+        halves = add_split(self.bits, parts)
+        new_state, new_left = [], []
+        for (send, keep), left, order in zip(halves, self.left, self.orders):
+            bit = order[self.stage]
+            new_state.append((keep, 0, swap(self.plan, send, bit), 0))
+            new_left.append(tuple(b for b in left if b != bit))
+        self.state, self.left = new_state, new_left
+        self.stage += 1
+
+    def last(self):
+        return [s[0] for s in self.state], [s[2] for s in self.state]
+
+
+def finish(plan, scatter, layouts):
+    kept, received = scatter.last()
+    m, rows = len(kept), scatter.rows
+
+    def body(*refs):
+        outs, total = refs[2 * m : -1], refs[-1]
+        for t in range(m):
+            total[t * rows : (t + 1) * rows, :] = refs[t][0].astype(F32) + refs[m + t][0].astype(F32)
+        for out, (first, span, tiles, used, folds) in zip(outs, layouts):
+            for j in range(tiles):
+                out[:, j * LANES : (j + 1) * LANES] = total[first + j * span : first + (j + 1) * span, :]
+            if used:
+                tile = total[first + tiles * span : first + tiles * span + span // folds, :]
+                for g in range(folds):
+                    moved = tile if g == 0 else pltpu.roll(tile, LANES - g * used, 1)
+                    here = slice(g * (span // folds), (g + 1) * (span // folds))
+                    out[here, tiles * LANES : tiles * LANES + used] = moved[:, :used]
+
+    block = whole((1, rows, LANES))
+    out_shape = [shape((span, tiles * LANES + used), F32) for _, span, tiles, used, _ in layouts]
+    return pl.pallas_call(
+        body,
+        grid=(1,),
+        in_specs=[block] * (2 * m),
+        out_specs=[whole(s.shape) for s in out_shape],
+        out_shape=out_shape,
+        scratch_shapes=[pltpu.VMEM((m * rows, LANES), F32)],
+        compiler_params=params(),
+        cost_estimate=cost(m * rows * LANES, 8 * m * rows * LANES),
+        name="finish",
+    )(*kept, *received)
+
+
+def fast_layer(
+    mesh,
+    block_input,
+    modulation,
+    frame_counts,
+    qkv_weight,
+    qv_bias,
+    out_weight,
+    out_bias,
+    fc1_weight,
+    fc1_bias,
+    fc2_weight,
+    fc2_bias,
+    out_cotangent,
+):
+    plan = Plan(mesh, block_input.shape, qkv_weight.shape, fc1_weight.shape)
+    n, width, rows = plan.frame_axis, plan.width, plan.rows
+    frame_at = lax.axis_index("frame").astype(jnp.int32)
+    clip_at = lax.axis_index("clip").astype(jnp.int32)
+    me = frame_at.reshape(1)
+    core = (clip_at % 2).reshape(1)
+    bits = jnp.stack([clip_at % 2, frame_at % 2, frame_at // 2, clip_at // 2 % 2, clip_at // 4])
+
+    slot = jnp.arange(plan.frames, dtype=jnp.int32)
+    frame_of = jnp.bitwise_xor(slot // plan.local_frames, frame_at) * plan.local_frames + slot % plan.local_frames
+    valid = frame_of[None, :] < frame_counts[:, None]
+    place = jnp.arange(plan.block, dtype=jnp.int32)
+    same = place[:, None] % 8 == place[None, :] % 8
+    allowed = same[None] & jnp.repeat(valid, 8, axis=1)[:, None, :]
+    score_mask = jnp.where(allowed, 0.0, NEGATIVE).astype(F32)
+    row_valid = jnp.broadcast_to(
+        valid.astype(F32)[:, None, :, None, None], (plan.clips, plan.halves, plan.frames, 8, LANES)
+    ).reshape(rows, LANES)
+    mods = modulation.astype(F32).reshape(plan.clips, 6, width)
+    bias_full = jnp.concatenate(
+        [qv_bias[:width], jnp.zeros((width,), BF16), qv_bias[width:]]
+    ).astype(F32)[None, :]
+
+    def line(vector):
+        return vector.astype(F32)[None, :]
+
+    inputs = exchange(plan, split_chunks(plan, me, block_input))
+    cotangents = exchange(plan, split_chunks(plan, me, out_cotangent))
+    saved = forward(
+        plan, inputs, mods, score_mask, qkv_weight, bias_full, out_weight, line(out_bias), fc1_weight, line(fc1_bias)
+    )
+    send2, keep2, d_branch, d_result, d_fc2_bias = fc2_grad(plan, core, cotangents, mods, row_valid, saved["act"])
+    two = Scatter(plan, bits, send2, keep2, ORDERS)
+    d_hidden, d_fc1_bias = hidden_grad(plan, d_branch, fc2_weight, saved["gp"])
+    two.advance()
+    send1, keep1 = fc1_grad(plan, core, saved["n2"], d_hidden)
+    one = Scatter(plan, bits, send1, keep1, ORDERS)
+    d_middle, d_att, d_context, d_mods_two, d_out_bias = middle_grad(
+        plan, d_hidden, fc1_weight, mods, saved["mid"], saved["att"], d_result, out_weight
+    )
+    one.advance()
+    two.advance()
+    d_proj, d_proj_sums = attention_grad(plan, saved["proj"], saved["probs"], d_context)
+    send0, keep0 = attention_weight_grads(plan, core, saved["n1"], saved["ctx"], d_proj, d_att)
+    zero = Scatter(plan, bits, send0, keep0, ORDERS)
+    *in_rows, d_mods_one = input_grad_rows(plan, d_proj, qkv_weight, mods, saved["x"], d_middle)
+    *out_rows, d_gate_two = output_rows(
+        plan, saved["act"], fc2_weight, line(fc2_bias), mods, saved["mid"], d_result, row_valid
+    )
+    block_output = join_chunks(plan, me, exchange(plan, out_rows))
+    input_grad = join_chunks(plan, me, exchange(plan, in_rows))
+    one.advance()
+    zero.advance()
+    two.advance()
+    one.advance()
+    zero.advance()
+    two.advance()
+    one.advance()
+    zero.advance()
+    zero.advance()
+
+    span2, span1 = plan.ff // plan.clip_axis, width // plan.clip_axis
+    (fc2_out,) = finish(plan, two, [(0, span2, 2, 32, 4)])
+    (fc1_out,) = finish(plan, one, [(0, span1, 9, 0, 1)])
+    qkv_out, out_out = finish(plan, zero, [(0, span1, 6, 96, 1), (7 * span1, span1, 2, 32, 3)])
+
+    d_modulation = jnp.concatenate([d_mods_one, d_mods_two, d_gate_two], axis=1).reshape(plan.clips, 6 * width)
+    sums = jnp.sum(d_proj_sums, axis=0)
+    small = [
+        d_modulation,
+        jnp.concatenate([sums[0], sums[2]])[None, :],
+        d_out_bias,
+        d_fc1_bias,
+        d_fc2_bias,
+    ]
+    cut = [v.reshape(v.shape[0], n, v.shape[1] // n) for v in small]
+    flat = jnp.concatenate([v.transpose(1, 0, 2).reshape(n, -1) for v in cut], axis=1)
+    at = [0]
+    for v in cut:
+        at.append(at[-1] + v.shape[0] * v.shape[2])
+    pieces = [lax.dynamic_index_in_dim(flat, jnp.bitwise_xor(frame_at, k), 0, keepdims=True) for k in range(n)]
+    mine = pieces[0]
+    for k in range(1, n):
+        mine = mine + lax.ppermute(pieces[k], "frame", [(i, i ^ k) for i in range(n)])
+    modulation_grad = mine[0, : at[1]].reshape(plan.clips, 6 * width // n)
+    biases = mine[:, at[1] :]
+    for bit in ("core", "z0", "z1"):
+        biases = biases + swap(plan, biases, bit)
+    biases = biases[0]
+    ends = [p - at[1] for p in at[1:]]
+    return (
+        block_output,
+        input_grad,
+        modulation_grad,
+        qkv_out,
+        biases[ends[0] : ends[1]],
+        out_out,
+        biases[ends[1] : ends[2]],
+        fc1_out,
+        biases[ends[2] : ends[3]],
+        fc2_out,
+        biases[ends[3] : ends[4]],
+    )
+
+
 def solution(mesh):
     placed = (
         P("clip", "frame", None, None),
@@ -235,8 +1202,13 @@
         P(),
         P("clip", "frame", None, None),
     )
+    def layer(*arrays):
+        if fits(mesh, arrays[0].shape, arrays[3].shape, arrays[7].shape):
+            return fast_layer(mesh, *arrays)
+        return on_device(*arrays)
+
     return jax.shard_map(
-        on_device,
+        layer,
         mesh=mesh,
         in_specs=placed,
         out_specs=(

time: 1030 us -> 496 us (0.48)
  waiting for transfers between devices: 669 us -> 178 us
  Pallas kernels: 0 us -> 240 us
  matrix products: 129 us -> 0 us
  local copies, waits for them, and re-layouts: 112 us -> 14.8 us
  blocking collectives: 52.1 us -> 0 us
  starting transfers between devices: 17.8 us -> 50.2 us
  other arithmetic: 31.5 us -> 2.42 us
  between operations: 16.9 us -> 1.34 us
    reduce_scatter x5 -> x0, waiting for transfers between devices: 499 us -> none  [the longest x1 187 us: on_device(): lax.psum_scatter(d_fc1_weight, 'frame', scatter_dimension=1, tiled=True)]
    pallas_call x0 -> x28, Pallas kernels: none -> 240 us  [the longest x12 63.1 us: add_split(): pl.pallas_call(body, grid_spec=pltpu.PrefetchScalarGridSpec(num_scalar_pr...]
    ppermute x0 -> x45, waiting for transfers between devices: none -> 178 us  [the longest x30 167 us: swap(): return lax.ppermute(value, axis, [(i, i ^ step) for i in range(size)])]
    unnamed x13 -> x0, waiting for transfers between devices: 136 us -> none
    dot_general x18 -> x0, matrix products: 129 us -> none  [the longest x4 40.8 us: contract_cols(): lax.dot_general(left, right, (((1,), (1,)), ((), ())), preferred_element_...]
    ppermute x0 -> x45, starting transfers between devices: none -> 50.2 us  [the longest x30 30.5 us: swap(): return lax.ppermute(value, axis, [(i, i ^ step) for i in range(size)])]
    unnamed x113 -> x101, local copies, waits for them, and re-layouts: 43.8 us -> 6.87 us
    convert_element_type x8 -> x0, local copies, waits for them, and re-layouts: 33.7 us -> none  [the longest x3 26.5 us: on_device(): d_projected = jnp.stack([d_queries, d_keys, d_values], axis=3).astype(jnp...]
  transfers between devices with their start and end apart: 13 -> 45, of which waited for: 10 -> 12; matrix products, arithmetic and copies ran while one was open for 22% -> 2% of each run, Pallas kernels for 0% -> 40%
where the time goes in v1:
time: 496 us; the launch traced here: 487 us
  Pallas kernels  240 us (48%)
  waiting for transfers between devices  178 us (36%)
  starting transfers between devices  50.2 us (10%)
  local copies, waits for them, and re-layouts  14.8 us (3%)
    ppermute x30, waiting for transfers between devices, swap(): return lax.ppermute(value, axis, [(i, i ^ step) for i in range(size)])  167 us
    pallas_call x12, Pallas kernels, add_split(): pl.pallas_call(body, grid_spec=pltpu.PrefetchScalarGridSpec(num_scalar_pr...  63.1 us
    pallas_call x1, Pallas kernels, forward(): pl.pallas_call(body, grid=(steps,), in_specs=[whole(plan.chunk_dims)] * n...  40.7 us
    ppermute x30, starting transfers between devices, swap(): return lax.ppermute(value, axis, [(i, i ^ step) for i in range(size)])  30.5 us
    pallas_call x1, Pallas kernels, middle_grad(): pl.pallas_call(body, grid=(steps,), in_specs=[pl.BlockSpec((rows, width),...  18.9 us
    pallas_call x1, Pallas kernels, attention_grad(): pl.pallas_call(body, grid=(plan.blocks,), in_specs=[pl.BlockSpec((3, bloc...  18.8 us
    pallas_call x1, Pallas kernels, attention_weight_grads(): pl.pallas_call(body, grid_spec=pltpu.PrefetchScalarGridSpec(num_scalar_pr...  16.9 us
    pallas_call x1, Pallas kernels, fc2_grad(): pl.pallas_call(body, grid_spec=pltpu.PrefetchScalarGridSpec(num_scalar_pr...  16.4 us
  transfers between devices with their start and end apart: 45, of which 12 were waited for; matrix products, arithmetic and copies ran while one was open for 2% of the time, Pallas kernels for 40%

profile of v1, /device:TPU:0, one launch (start us, length us, event | category | flops | bytes accessed | tf_op | source)
XLA Modules:
  0.0 486.7 jit_solution(9530648194147338766)
XLA Ops:
  0.6 2.3 split_chunks.2
  2.9 2.9 collective-permute-start
  5.8 1.5 collective-permute-start.1
  7.5 2.3 split_chunks.3
  9.7 1.9 collective-permute-start.3
  11.7 1.5 collective-permute-start.4
  17.0 5.1 %collective-permute-done.1.refs_2_ = bf16[2,2,4,8,1152]{4,3,2,1,0:T(8,128)(2,1)S(1)} collective-permute-done((bf16[2,2,4,8,1152]{4,3,2,1,0:T(8,128)(2,1)}, bf16[2,2,4,8,1152]{4,3,2,1,0:T(8,128)(2,1)S(1)}, u32[]{:S(2)}, u32[]{:S(2)}) %collective-permute-start.1) | collective-permute-done | bytes 294944 | tf_op jit(solution)/shard_map/ppermute | solution.py:384
  23.0 40.7 %forward.1 = (f32[4,16,128,128]{3,2,1,0:T(8,128)}, f32[512,4608]{1,0:T(8,128)}, bf16[512,4608]{1,0:T(8,128)(2,1)}, f32[512,1152]{1,0:T(8,128)}, bf16[512,1152]{1...) custom-call(bf16[2,2,4,8,1152]{4,3,2,1,0:T(8,128)(2,1)} %get-tuple-e, ...), custom_call_target="tpu_custom_call" | custom-call | flops 17999998976 | bytes 60000000 | tf_op jit(solution)/shard_map/forward/pallas_call | solution.py:486
  64.7 16.4 %fc2_grad.1 = (bf16[4,4,1296,128]{3,2,1,0:T(8,128)(2,1)}, bf16[4,4,1296,128]{3,2,1,0:T(8,128)(2,1)}, bf16[512,1152]{1,0:T(8,128)(2,1)}, bf16[512,1152]{1,0:T(8,128)(2,1)}, f32[1,1152]{1,0:T(1,128)}) custom-call(s32[1]{0:T(128)} %bitcast.1.core_ref, bf16[2,2,4,8,1152]{4,3,2,1,0:T(8,128)(2,1)} %get-tuple-element.113.refs_0_, ...), custom_call_target="tpu_custom_call" | custom-call | flops 7000000000 | bytes 20000000 | tf_op jit(solution)/shard_map/fc2_grad/pallas_call | solution.py:584
  81.1 13.4 %hidden_grad.1 = (bf16[512,4608]{1,0:T(8,128)(2,1)}, f32[1,4608]{1,0:T(1,128)}) custom-call(bf16[512,1152]{1,0:T(8,128)(2,1)} %get-tuple-element.124.dbr, bf16[4608,1152]{1,0:T(8,128)(2,1)} %w2.1, f32[512,4608]{1,0:T(8,128)} %get-tuple-element.125.slope), custom_call_target="tpu_custom_call" | custom-call | flops 5400000000 | bytes 26000000 | tf_op jit(solution)/shard_map/hidden_grad/pallas_call | solution.py:619
  94.5 11.6 %fc1_grad.1 = (bf16[4,4,1296,128]{3,2,1,0:T(8,128)(2,1)}, bf16[4,4,1296,128]{3,2,1,0:T(8,128)(2,1)}) custom-call(s32[1]{0:T(128)} %bitcast.1.core_ref, bf16[512,1152]{1,0:T(8,128)(2,1)} %get-tuple-element.166.left, bf16[512,4608]{1,0:T(8,128)(2,1)} %get-tuple-element.126.dh), custom_call_target="tpu_custom_call" | custom-call | flops 5400000000 | bytes 17000000 | tf_op jit(solution)/shard_map/fc1_grad/pallas_call | solution.py:654
  106.2 18.9 %middle_grad.1 = (f32[512,1152]{1,0:T(8,128)}, bf16[512,1152]{1,0:T(8,128)(2,1)}, bf16[512,1152]{1,0:T(8,128)(2,1)}, f32[2,3,1152]{2,1,0:T(4,128)}, f32[1,1152]{1,0:T(1,128)}) custom-call(bf16[512,4608]{1,0:T(8,128)(2,1)} %get-tuple-element.126.dh, bf16[1152,4608]{1,0:T(8,128)(2,1)} %w1.1, f32[2,6,1152]{2,1,0:T(8,128)} %reshape.219.refs_4_.mod, ...), custom_call_target="tpu_custom_call" | custom-call | flops 7000000000 | bytes 30000000 | tf_op jit(solution)/shard_map/middle_grad/pallas_call | solution.py:703
  125.1 18.8 %attention_grad.1 = (bf16[3,512,1152]{2,1,0:T(8,128)(2,1)}, f32[4,3,1152]{2,1,0:T(4,128)}) custom-call(bf16[3,512,1152]{2,1,0:T(8,128)(2,1)} %get-tuple-element.122.p, f32[4,16,128,128]{3,2,1,0:T(8,128)} %get-tuple-element.123.w, bf16[512,1152]{1,0:T(8,128)(2,1)} %get-tuple-element.128.dctx), custom_call_target="tpu_custom_call" | custom-call | flops 4000000000 | bytes 14000000 | tf_op jit(solution)/shard_map/attention_grad/pallas_call | solution.py:761
  143.9 16.9 %attention_weight_grads.1 = (bf16[4,4,1344,128]{3,2,1,0:T(8,128)(2,1)}, bf16[4,4,1344,128]{3,2,1,0:T(8,128)(2,1)}) custom-call(s32[1]{0:T(128)} %bitcast.1.core_ref, bf16[512,1152]{1,0:T(8,128)(2,1)} %get-tuple-element.143.left_q, bf16[512,1152]{1,0:T(8,128)(2,1)} %get-tuple-element.144.left_o, bf16[3,512,1152]{2,1,0:T(8,128)(2,1)} %get-tuple-element.129.dp, ...), custom_call_target="tpu_custom_call" | custom-call | flops 6000000000 | bytes 18000000 | tf_op jit(solution)/shard_map/attention_weight_grads/pallas_call | solution.py:825
  162.6 12.7 %output_rows.1 = (bf16[2,2,4,8,1152]{4,3,2,1,0:T(8,128)(2,1)}, bf16[2,2,4,8,1152]{4,3,2,1,0:T(8,128)(2,1)}, bf16[2,2,4,8,1152]{4,3,2,1,0:T(8,128)(2,1)}, bf16[2,...) custom-call(bf16[512,4608]{1,0:T(8,128)(2,1)} %get-tuple-element.111.refs_6_.a, bf16[4608,1152]{1,0:T(8,128)(2,1)} %w2.1, ...), custom_call_target="tpu_custom_call" | custom-call | flops 5400000000 | bytes 26000000 | tf_op jit(solution)/shard_map/output_rows/pallas_call | solution.py:931
  175.3 9.1 %add_split.16 = (bf16[8,648,128]{2,1,0:T(8,128)(2,1)}, bf16[8,648,128]{2,1,0:T(8,128)(2,1)}, bf16[8,648,128]{2,1,0:T(8,128)(2,1)}, bf16[8,648,128]{2,1,0:T(8,128)(2,1)}) custom-call(s32[5]{0:T(128)} %stack.20.bits_ref, bf16[16,1296,128]{2,1,0:T(8,128)(2,1)} %bitcast.23, bf16[16,1296,128]{2,1,0:T(8,128)(2,1)} %bitcast.24, ...), custom_call_target="tpu_custom_call" | custom-call | flops 3981312 | bytes 15925248 | tf_op jit(solution)/shard_map/add_split/pallas_call | solution.py:995
  184.4 1.1 collective-permute-start.28
  185.5 12.3 %input_grad_rows.1 = (bf16[2,2,4,8,1152]{4,3,2,1,0:T(8,128)(2,1)}, bf16[2,2,4,8,1152]{4,3,2,1,0:T(8,128)(2,1)}, bf16[2,2,4,8,1152]{4,3,2,1,0:T(8,128)(2,1)}, bf1...) custom-call(bf16[3,512,1152]{2,1,0:T(8,128)(2,1)} %get-tuple-element.129.dp, bf16[1152,3456]{1,0:T(8,128)(2,1)} %w.3, ...), custom_call_target="tpu_custom_call" | custom-call | flops 4000000000 | bytes 20000000 | tf_op jit(solution)/shard_map/input_grad_rows/pallas_call | solution.py:883
  199.6 2.2 collective-permute-start.14
  202.2 1.0 collective-permute-start.12
  203.2 9.3 %add_split.12 = (bf16[8,672,128]{2,1,0:T(8,128)(2,1)}, bf16[8,672,128]{2,1,0:T(8,128)(2,1)}, bf16[8,672,128]{2,1,0:T(8,128)(2,1)}, bf16[8,672,128]{2,1,0:T(8,128)(2,1)}) custom-call(s32[5]{0:T(128)} %stack.20.bits_ref, bf16[16,1344,128]{2,1,0:T(8,128)(2,1)} %bitcast.15, bf16[16,1344,128]{2,1,0:T(8,128)(2,1)} %bitcast.16, ...), custom_call_target="tpu_custom_call" | custom-call | flops 4128768 | bytes 16515072 | tf_op jit(solution)/shard_map/add_split/pallas_call | solution.py:995
  212.5 5.6 %collective-permute-done.14 = f32[1,5760]{1,0:T(1,128)S(1)} collective-permute-done((f32[1,5760]{1,0:T(1,128)S(1)}, f32[1,5760]{1,0:T(1,128)S(1)}, u32[]{:S(2)}, u32[]{:S(2)}) %collective-permute-start.14) | collective-permute-done | bytes 23072 | tf_op jit(solution)/shard_map/ppermute | solution.py:1168
  219.4 9.1 %add_split.20 = (bf16[8,648,128]{2,1,0:T(8,128)(2,1)}, bf16[8,648,128]{2,1,0:T(8,128)(2,1)}, bf16[8,648,128]{2,1,0:T(8,128)(2,1)}, bf16[8,648,128]{2,1,0:T(8,128)(2,1)}) custom-call(s32[5]{0:T(128)} %stack.20.bits_ref, bf16[16,1296,128]{2,1,0:T(8,128)(2,1)} %bitcast.19, bf16[16,1296,128]{2,1,0:T(8,128)(2,1)} %bitcast.20, ...), custom_call_target="tpu_custom_call" | custom-call | flops 3981312 | bytes 15925248 | tf_op jit(solution)/shard_map/add_split/pallas_call | solution.py:995
  228.5 1.1 collective-permute-start.29
  229.6 1.6 collective-permute-start.37
  231.7 48.6 %collective-permute-done.29.refs_6_.refs_7_ = bf16[8,648,128]{2,1,0:T(8,128)(2,1)} collective-permute-done((bf16[8,648,128]{2,1,0:T(8,128)(2,1)}, bf16[8,648,128]{2,1,0:T(8,128)(2,1)}, u32[]{:S(2)}, u32[]{:S(2)}) %collective-permute-start.29) | collective-permute-done | bytes 1327136 | tf_op jit(solution)/shard_map/ppermute | solution.py:960
  280.3 5.3 %add_split.17 = (bf16[4,648,128]{2,1,0:T(8,128)(2,1)}, bf16[4,648,128]{2,1,0:T(8,128)(2,1)}, bf16[4,648,128]{2,1,0:T(8,128)(2,1)}, bf16[4,648,128]{2,1,0:T(8,128)(2,1)}) custom-call(s32[5]{0:T(128)} %stack.20.bits_ref, bf16[8,648,128]{2,1,0:T(8,128)(2,1)} %get-tuple-element.169.refs_0_.refs_1_, bf16[8,648,128]{2,1,0:T(8,128)(2,1)} %get-tuple-element.169.refs_0_.refs_1_, ...), custom_call_target="tpu_custom_call" | custom-call | flops 1990656 | bytes 7962624 | tf_op jit(solution)/shard_map/add_split/pallas_call | solution.py:995
  285.7 1.6 collective-permute-start.30
  288.4 5.4 %add_split.13 = (bf16[4,672,128]{2,1,0:T(8,128)(2,1)}, bf16[4,672,128]{2,1,0:T(8,128)(2,1)}, bf16[4,672,128]{2,1,0:T(8,128)(2,1)}, bf16[4,672,128]{2,1,0:T(8,128)(2,1)}) custom-call(s32[5]{0:T(128)} %stack.20.bits_ref, bf16[8,672,128]{2,1,0:T(8,128)(2,1)} %get-tuple-element.148.refs_0_.refs_1_, bf16[8,672,128]{2,1,0:T(8,128)(2,1)} %get-tuple-element.148.refs_0_.refs_1_, ...), custom_call_target="tpu_custom_call" | custom-call | flops 2064384 | bytes 8257536 | tf_op jit(solution)/shard_map/add_split/pallas_call | solution.py:995
  294.8 1.1 collective-permute-start.19
  295.9 10.6 %collective-permute-done.38.refs_6_.refs_7_ = bf16[8,648,128]{2,1,0:T(8,128)(2,1)S(1)} collective-permute-done((bf16[8,648,128]{2,1,0:T(8,128)(2,1)}, bf16[8,648,128]{2,1,0:T(8,128)(2,1)S(1)}, u32[]{:S(2)}, u32[]{:S(2)}) %collective-permute-start.38) | collective-permute-done | bytes 1327136 | tf_op jit(solution)/shard_map/ppermute | solution.py:960
  306.5 1.6 collective-permute-start.25
  308.1 5.4 %add_split.21 = (bf16[4,648,128]{2,1,0:T(8,128)(2,1)}, bf16[4,648,128]{2,1,0:T(8,128)(2,1)}, bf16[4,648,128]{2,1,0:T(8,128)(2,1)}, bf16[4,648,128]{2,1,0:T(8,128)(2,1)}) custom-call(s32[5]{0:T(128)} %stack.20.bits_ref, bf16[8,648,128]{2,1,0:T(8,128)(2,1)} %get-tuple-element.187.refs_0_.refs_1_, bf16[8,648,128]{2,1,0:T(8,128)(2,1)} %get-tuple-element.187.refs_0_.refs_1_, ...), custom_call_target="tpu_custom_call" | custom-call | flops 1990656 | bytes 7962624 | tf_op jit(solution)/shard_map/add_split/pallas_call | solution.py:995
  313.4 33.7 %collective-permute-done.25 = f32[1,2304]{1,0:T(1,128)S(1)} collective-permute-done((f32[1,2304]{1,0:T(1,128)S(1)}, f32[1,2304]{1,0:T(1,128)S(1)}, u32[]{:S(2)}, u32[]{:S(2)}) %collective-permute-start.25) | collective-permute-done | bytes 9248 | tf_op jit(solution)/shard_map/ppermute | solution.py:960
  347.2 1.6 collective-permute-start.39
  349.2 1.6 collective-permute-start.6
  351.2 3.5 add_split.18
  354.7 2.6 collective-permute-start.32
  357.3 3.5 add_split.14
  360.8 11.5 %collective-permute-done.39.refs_2_.refs_3_ = bf16[4,648,128]{2,1,0:T(8,128)(2,1)S(1)} collective-permute-done((bf16[4,648,128]{2,1,0:T(8,128)(2,1)}, bf16[4,648,128]{2,1,0:T(8,128)(2,1)S(1)}, u32[]{:S(2)}, u32[]{:S(2)}) %collective-permute-start.39) | collective-permute-done | bytes 663584 | tf_op jit(solution)/shard_map/ppermute | solution.py:960
  372.3 1.8 collective-permute-start.20
  374.1 17.8 %collective-permute-done.40.refs_6_.refs_7_ = bf16[4,648,128]{2,1,0:T(8,128)(2,1)S(1)} collective-permute-done((bf16[4,648,128]{2,1,0:T(8,128)(2,1)}, bf16[4,648,128]{2,1,0:T(8,128)(2,1)S(1)}, u32[]{:S(2)}, u32[]{:S(2)}) %collective-permute-start.40) | collective-permute-done | bytes 663584 | tf_op jit(solution)/shard_map/ppermute | solution.py:960
  392.7 3.6 add_split.22
  396.4 2.0 collective-permute-start.33
  399.4 2.0 collective-permute-start.42
  402.4 32.6 %collective-permute-done.33.refs_6_.refs_7_ = bf16[2,648,128]{2,1,0:T(8,128)(2,1)S(1)} collective-permute-done((bf16[2,648,128]{2,1,0:T(8,128)(2,1)S(1)}, bf16[2,648,128]{2,1,0:T(8,128)(2,1)S(1)}, u32[]{:S(2)}, u32[]{:S(2)}) %collective-permute-start.33) | collective-permute-done | bytes 331808 | tf_op jit(solution)/shard_map/ppermute | solution.py:960
  434.9 1.4 collective-permute-start.8
  436.3 5.7 %collective-permute-done.41.refs_2_.refs_3_ = bf16[2,648,128]{2,1,0:T(8,128)(2,1)S(1)} collective-permute-done((bf16[2,648,128]{2,1,0:T(8,128)(2,1)}, bf16[2,648,128]{2,1,0:T(8,128)(2,1)S(1)}, u32[]{:S(2)}, u32[]{:S(2)}) %collective-permute-start.41) | collective-permute-done | bytes 331808 | tf_op jit(solution)/shard_map/ppermute | solution.py:960
  442.1 1.6 collective-permute-start.9
  443.7 5.5 %collective-permute-done.42.refs_6_.refs_7_ = bf16[2,648,128]{2,1,0:T(8,128)(2,1)S(1)} collective-permute-done((bf16[2,648,128]{2,1,0:T(8,128)(2,1)}, bf16[2,648,128]{2,1,0:T(8,128)(2,1)S(1)}, u32[]{:S(2)}, u32[]{:S(2)}) %collective-permute-start.42) | collective-permute-done | bytes 331808 | tf_op jit(solution)/shard_map/ppermute | solution.py:960
  450.1 2.1 collective-permute-start.11
  452.3 2.9 add_split.19
  456.1 1.0 collective-permute-start.34
  458.6 2.9 add_split.23
  461.5 3.1 add_split.15
  464.6 1.1 collective-permute-start.35
  465.7 1.8 collective-permute-start.43
  468.9 1.0 collective-permute-start.23
  471.2 2.2 join_chunks.2
  473.5 2.2 join_chunks.3
  476.4 2.1 finish.4
  479.1 2.2 finish.5
  481.4 2.3 copy.25
  484.4 2.1 finish.3
  (203 shorter events, 25.2 us)
Async XLA Ops:
  2.9 14.1 %collective-permute-start = (bf16[2,2,4,8,1152]{4,3,2,1,0:T(8,128)(2,1)}, bf16[2,2,4,8,1152]{4,3,2,1,0:T(8,128)(2,1)S(1)}, u32[]{:S(2)}, u32[]{:S(2)}) collective-permute-start(bf16[2,2,4,8,1152]{4,3,2,1,0:T(8,128)(2,1)} %get-tuple-element.108), channel_id=1, source_target_pairs={{0,1},{1,0},{2,3},{3,2},{4,5},{5,4},{6,7},{7,6},{8,9},{9,8},{10,11... | collective-permute-start | bytes 884744 | tf_op jit(solution)/shard_map/ppermute | solution.py:384
  5.8 16.3 %collective-permute-start.1 = (bf16[2,2,4,8,1152]{4,3,2,1,0:T(8,128)(2,1)}, bf16[2,2,4,8,1152]{4,3,2,1,0:T(8,128)(2,1)S(1)}, u32[]{:S(2)}, u32[]{:S(2)}) collective-permute-start(bf16[2,2,4,8,1152]{4,3,2,1,0:T(8,128)(2,1)} %get-tuple-element.109), channel_id=1, source_target_pairs={{0,2},{1,3},{2,0},{3,1},{4,6},{5,7},{6,4},{7,5},{8,10},{9,11},{10,... | collective-permute-start | bytes 884744 | tf_op jit(solution)/shard_map/ppermute | solution.py:384
  7.4 8.1 %copy-start.32 = (bf16[4608]{0:T(1024)(128)(2,1)S(1)}, bf16[4608]{0:T(1024)(128)(2,1)}, u32[]{:S(2)}) copy-start(bf16[4608]{0:T(1024)(128)(2,1)} %param.20) | copy-start | bytes 27652
  7.4 14.8 %collective-permute-start.2 = (bf16[2,2,4,8,1152]{4,3,2,1,0:T(8,128)(2,1)}, bf16[2,2,4,8,1152]{4,3,2,1,0:T(8,128)(2,1)S(1)}, u32[]{:S(2)}, u32[]{:S(2)}) collective-permute-start(bf16[2,2,4,8,1152]{4,3,2,1,0:T(8,128)(2,1)} %get-tuple-element.110), channel_id=1, source_target_pairs={{0,3},{1,2},{2,1},{3,0},{4,7},{5,6},{6,5},{7,4},{8,11},{9,10},{10,... | collective-permute-start | bytes 884744 | tf_op jit(solution)/shard_map/ppermute | solution.py:384
  9.7 53.9 %collective-permute-start.3 = (bf16[2,2,4,8,1152]{4,3,2,1,0:T(8,128)(2,1)}, bf16[2,2,4,8,1152]{4,3,2,1,0:T(8,128)(2,1)S(1)}, u32[]{:S(2)}, u32[]{:S(2)}) collective-permute-start(bf16[2,2,4,8,1152]{4,3,2,1,0:T(8,128)(2,1)} %get-tuple-element.114), channel_id=1, source_target_pairs={{0,1},{1,0},{2,3},{3,2},{4,5},{5,4},{6,7},{7,6},{8,9},{9,8},{10,11... | collective-permute-start | bytes 884744 | tf_op jit(solution)/shard_map/ppermute | solution.py:384
  11.7 52.0 %collective-permute-start.4 = (bf16[2,2,4,8,1152]{4,3,2,1,0:T(8,128)(2,1)}, bf16[2,2,4,8,1152]{4,3,2,1,0:T(8,128)(2,1)S(1)}, u32[]{:S(2)}, u32[]{:S(2)}) collective-permute-start(bf16[2,2,4,8,1152]{4,3,2,1,0:T(8,128)(2,1)} %get-tuple-element.115), channel_id=1, source_target_pairs={{0,2},{1,3},{2,0},{3,1},{4,6},{5,7},{6,4},{7,5},{8,10},{9,11},{10,... | collective-permute-start | bytes 884744 | tf_op jit(solution)/shard_map/ppermute | solution.py:384
  17.0 46.8 %collective-permute-start.5 = (bf16[2,2,4,8,1152]{4,3,2,1,0:T(8,128)(2,1)}, bf16[2,2,4,8,1152]{4,3,2,1,0:T(8,128)(2,1)S(1)}, u32[]{:S(2)}, u32[]{:S(2)}) collective-permute-start(bf16[2,2,4,8,1152]{4,3,2,1,0:T(8,128)(2,1)} %get-tuple-element.116), channel_id=1, source_target_pairs={{0,3},{1,2},{2,1},{3,0},{4,7},{5,6},{6,5},{7,4},{8,11},{9,10},{10,... | collective-permute-start | bytes 884744 | tf_op jit(solution)/shard_map/ppermute | solution.py:384
  106.2 69.1 %collective-permute-start.27 = (bf16[16,1296,128]{2,1,0:T(8,128)(2,1)}, bf16[16,1296,128]{2,1,0:T(8,128)(2,1)}, u32[]{:S(2)}, u32[]{:S(2)}) collective-permute-start(bf16[16,1296,128]{2,1,0:T(8,128)(2,1)} %bitcast.30), channel_id=1, source_target_pairs={{0,4},{4,0},{8,12},{12,8},{16,20},{20,16},{24,28},{28,24},{1,5},{5... | collective-permute-start | bytes 15925256 | tf_op jit(solution)/shard_map/ppermute | solution.py:960
  143.9 17.5 %copy-start.37 = (bf16[1152]{0:T(1024)(128)(2,1)S(1)}, bf16[1152]{0:T(1024)(128)(2,1)}, u32[]{:S(2)}) copy-start(bf16[1152]{0:T(1024)(128)(2,1)} %param.22) | copy-start | bytes 6916
  160.8 41.3 %collective-permute-start.15 = (bf16[16,1344,128]{2,1,0:T(8,128)(2,1)}, bf16[16,1344,128]{2,1,0:T(8,128)(2,1)}, u32[]{:S(2)}, u32[]{:S(2)}) collective-permute-start(bf16[16,1344,128]{2,1,0:T(8,128)(2,1)} %bitcast.28), channel_id=1, source_target_pairs={{0,4},{4,0},{8,12},{12,8},{16,20},{20,16},{24,28},{28,24},{1,5},{5... | collective-permute-start | bytes 16515080 | tf_op jit(solution)/shard_map/ppermute | solution.py:960
  161.3 57.2 %collective-permute-start.36 = (bf16[16,1296,128]{2,1,0:T(8,128)(2,1)}, bf16[16,1296,128]{2,1,0:T(8,128)(2,1)}, u32[]{:S(2)}, u32[]{:S(2)}) collective-permute-start(bf16[16,1296,128]{2,1,0:T(8,128)(2,1)} %bitcast.29), channel_id=1, source_target_pairs={{0,4},{4,0},{8,12},{12,8},{16,20},{20,16},{24,28},{28,24},{1,5},{5... | collective-permute-start | bytes 15925256 | tf_op jit(solution)/shard_map/ppermute | solution.py:960
  184.4 46.9 %collective-permute-start.28 = (bf16[8,648,128]{2,1,0:T(8,128)(2,1)}, bf16[8,648,128]{2,1,0:T(8,128)(2,1)}, u32[]{:S(2)}, u32[]{:S(2)}) collective-permute-start(bf16[8,648,128]{2,1,0:T(8,128)(2,1)} %get-tuple-element.170), channel_id=1, source_target_pairs={{0,1},{1,0},{2,3},{3,2},{4,5},{5,4},{6,7},{7,6},{8,9},{9,8},{10,11... | collective-permute-start | bytes 3981320 | tf_op jit(solution)/shard_map/ppermute | solution.py:960
  185.5 12.4 %copy-start.28 = (f32[2,3,1152]{2,1,0:T(4,128)S(1)}, f32[2,3,1152]{2,1,0:T(4,128)}, u32[]{:S(2)}) copy-start(f32[2,3,1152]{2,1,0:T(4,128)} %get-tuple-element.137) | copy-start | bytes 82948
  185.5 12.4 %copy-start.33 = (f32[2,1,1152]{2,1,0:T(1,128)S(1)}, f32[2,1,1152]{2,1,0:T(1,128)}, u32[]{:S(2)}) copy-start(f32[2,1,1152]{2,1,0:T(1,128)} %get-tuple-element.138) | copy-start | bytes 27652
  185.5 13.4 %copy-start.27 = (f32[4,3,1152]{2,1,0:T(4,128)S(1)}, f32[4,3,1152]{2,1,0:T(4,128)}, u32[]{:S(2)}) copy-start(f32[4,3,1152]{2,1,0:T(4,128)} %get-tuple-element.139) | copy-start | bytes 165892
  185.5 13.6 %copy-start.35 = (f32[1,1152]{1,0:T(1,128)S(1)}, f32[1,1152]{1,0:T(1,128)}, u32[]{:S(2)}) copy-start(f32[1,1152]{1,0:T(1,128)} %get-tuple-element.140) | copy-start | bytes 13828
  185.5 13.7 %copy-start.30 = (f32[1,4608]{1,0:T(1,128)S(1)}, f32[1,4608]{1,0:T(1,128)}, u32[]{:S(2)}) copy-start(f32[1,4608]{1,0:T(1,128)} %get-tuple-element.141) | copy-start | bytes 55300
  185.5 13.8 %copy-start.34 = (f32[1,1152]{1,0:T(1,128)S(1)}, f32[1,1152]{1,0:T(1,128)}, u32[]{:S(2)}) copy-start(f32[1,1152]{1,0:T(1,128)} %get-tuple-element.142) | copy-start | bytes 13828
  199.6 18.4 %collective-permute-start.14 = (f32[1,5760]{1,0:T(1,128)S(1)}, f32[1,5760]{1,0:T(1,128)S(1)}, u32[]{:S(2)}, u32[]{:S(2)}) collective-permute-start(f32[1,5760]{1,0:T(1,128)S(1)} %get-tuple-element.232), channel_id=1, source_target_pairs={{0,3},{1,2},{2,1},{3,0},{4,7},{5,6},{6,5},{7,4},{8,11},{9,10},{10,... | collective-permute-start | bytes 69128 | tf_op jit(solution)/shard_map/ppermute | solution.py:1168
  201.8 26.7 %collective-permute-start.13 = (f32[1,5760]{1,0:T(1,128)S(1)}, f32[1,5760]{1,0:T(1,128)S(1)}, u32[]{:S(2)}, u32[]{:S(2)}) collective-permute-start(f32[1,5760]{1,0:T(1,128)S(1)} %get-tuple-element.233), channel_id=1, source_target_pairs={{0,2},{1,3},{2,0},{3,1},{4,6},{5,7},{6,4},{7,5},{8,10},{9,11},{10,... | collective-permute-start | bytes 69128 | tf_op jit(solution)/shard_map/ppermute | solution.py:1168
  202.2 27.5 %collective-permute-start.12 = (f32[1,5760]{1,0:T(1,128)S(1)}, f32[1,5760]{1,0:T(1,128)S(1)}, u32[]{:S(2)}, u32[]{:S(2)}) collective-permute-start(f32[1,5760]{1,0:T(1,128)S(1)} %get-tuple-element.231), channel_id=1, source_target_pairs={{0,1},{1,0},{2,3},{3,2},{4,5},{5,4},{6,7},{7,6},{8,9},{9,8},{10,11... | collective-permute-start | bytes 69128 | tf_op jit(solution)/shard_map/ppermute | solution.py:1168
  218.0 67.6 %collective-permute-start.16 = (bf16[8,672,128]{2,1,0:T(8,128)(2,1)}, bf16[8,672,128]{2,1,0:T(8,128)(2,1)S(1)}, u32[]{:S(2)}, u32[]{:S(2)}) collective-permute-start(bf16[8,672,128]{2,1,0:T(8,128)(2,1)} %get-tuple-element.149), channel_id=1, source_target_pairs={{0,1},{1,0},{2,3},{3,2},{4,5},{5,4},{6,7},{7,6},{8,9},{9,8},{10,11... | collective-permute-start | bytes 4128776 | tf_op jit(solution)/shard_map/ppermute | solution.py:960
  218.4 68.9 %collective-permute-start.17 = (bf16[8,672,128]{2,1,0:T(8,128)(2,1)}, bf16[8,672,128]{2,1,0:T(8,128)(2,1)S(1)}, u32[]{:S(2)}, u32[]{:S(2)}) collective-permute-start(bf16[8,672,128]{2,1,0:T(8,128)(2,1)} %get-tuple-element.151), channel_id=1, source_target_pairs={{0,2},{1,3},{2,0},{3,1},{4,6},{5,7},{6,4},{7,5},{8,10},{9,11},{10,... | collective-permute-start | bytes 4128776 | tf_op jit(solution)/shard_map/ppermute | solution.py:960
  228.5 51.8 %collective-permute-start.29 = (bf16[8,648,128]{2,1,0:T(8,128)(2,1)}, bf16[8,648,128]{2,1,0:T(8,128)(2,1)}, u32[]{:S(2)}, u32[]{:S(2)}) collective-permute-start(bf16[8,648,128]{2,1,0:T(8,128)(2,1)} %get-tuple-element.172), channel_id=1, source_target_pairs={{0,2},{1,3},{2,0},{3,1},{4,6},{5,7},{6,4},{7,5},{8,10},{9,11},{10,... | collective-permute-start | bytes 3981320 | tf_op jit(solution)/shard_map/ppermute | solution.py:960
  229.6 65.2 %collective-permute-start.37 = (bf16[8,648,128]{2,1,0:T(8,128)(2,1)}, bf16[8,648,128]{2,1,0:T(8,128)(2,1)S(1)}, u32[]{:S(2)}, u32[]{:S(2)}) collective-permute-start(bf16[8,648,128]{2,1,0:T(8,128)(2,1)} %get-tuple-element.188), channel_id=1, source_target_pairs={{0,1},{1,0},{2,3},{3,2},{4,5},{5,4},{6,7},{7,6},{8,9},{9,8},{10,11... | collective-permute-start | bytes 3981320 | tf_op jit(solution)/shard_map/ppermute | solution.py:960
  231.3 75.2 %collective-permute-start.38 = (bf16[8,648,128]{2,1,0:T(8,128)(2,1)}, bf16[8,648,128]{2,1,0:T(8,128)(2,1)S(1)}, u32[]{:S(2)}, u32[]{:S(2)}) collective-permute-start(bf16[8,648,128]{2,1,0:T(8,128)(2,1)} %get-tuple-element.190), channel_id=1, source_target_pairs={{0,2},{1,3},{2,0},{3,1},{4,6},{5,7},{6,4},{7,5},{8,10},{9,11},{10,... | collective-permute-start | bytes 3981320 | tf_op jit(solution)/shard_map/ppermute | solution.py:960
  280.3 13.5 %collective-permute-start.24 = (f32[1,2304]{1,0:T(1,128)S(1)}, f32[1,2304]{1,0:T(1,128)S(1)}, u32[]{:S(2)}, u32[]{:S(2)}) collective-permute-start(f32[1,2304]{1,0:T(1,128)S(1)} %slice.59), channel_id=1, source_target_pairs={{0,4},{4,0},{8,12},{12,8},{16,20},{20,16},{24,28},{28,24},{1,5},{5... | collective-permute-start | bytes 27656 | tf_op jit(solution)/shard_map/ppermute | solution.py:960
  285.7 63.1 %collective-permute-start.30 = (bf16[4,648,128]{2,1,0:T(8,128)(2,1)}, bf16[4,648,128]{2,1,0:T(8,128)(2,1)S(1)}, u32[]{:S(2)}, u32[]{:S(2)}) collective-permute-start(bf16[4,648,128]{2,1,0:T(8,128)(2,1)} %get-tuple-element.174), channel_id=1, source_target_pairs={{0,8},{4,12},{8,0},{12,4},{16,24},{20,28},{24,16},{28,20},{1,9},{5... | collective-permute-start | bytes 1990664 | tf_op jit(solution)/shard_map/ppermute | solution.py:960
  287.3 61.9 %collective-permute-start.31 = (bf16[4,648,128]{2,1,0:T(8,128)(2,1)}, bf16[4,648,128]{2,1,0:T(8,128)(2,1)}, u32[]{:S(2)}, u32[]{:S(2)}) collective-permute-start(bf16[4,648,128]{2,1,0:T(8,128)(2,1)} %get-tuple-element.176), channel_id=1, source_target_pairs={{0,8},{4,12},{8,0},{12,4},{16,24},{20,28},{24,16},{28,20},{1,9},{5... | collective-permute-start | bytes 1990664 | tf_op jit(solution)/shard_map/ppermute | solution.py:960
  293.8 57.0 %collective-permute-start.18 = (bf16[4,672,128]{2,1,0:T(8,128)(2,1)}, bf16[4,672,128]{2,1,0:T(8,128)(2,1)S(1)}, u32[]{:S(2)}, u32[]{:S(2)}) collective-permute-start(bf16[4,672,128]{2,1,0:T(8,128)(2,1)} %get-tuple-element.153), channel_id=1, source_target_pairs={{0,8},{4,12},{8,0},{12,4},{16,24},{20,28},{24,16},{28,20},{1,9},{5... | collective-permute-start | bytes 2064392 | tf_op jit(solution)/shard_map/ppermute | solution.py:960
  294.8 13.2 %copy-start.2 = (bf16[8,648,128]{2,1,0:T(8,128)(2,1)}, bf16[8,648,128]{2,1,0:T(8,128)(2,1)S(1)}, u32[]{:S(2)}) copy-start(bf16[8,648,128]{2,1,0:T(8,128)(2,1)S(1)} %collective-permute-done.37.refs_2_.refs_3_) | copy-start | bytes 3981316
  294.8 59.8 %collective-permute-start.19 = (bf16[4,672,128]{2,1,0:T(8,128)(2,1)}, bf16[4,672,128]{2,1,0:T(8,128)(2,1)S(1)}, u32[]{:S(2)}, u32[]{:S(2)}) collective-permute-start(bf16[4,672,128]{2,1,0:T(8,128)(2,1)} %get-tuple-element.155), channel_id=1, source_target_pairs={{0,8},{4,12},{8,0},{12,4},{16,24},{20,28},{24,16},{28,20},{1,9},{5... | collective-permute-start | bytes 2064392 | tf_op jit(solution)/shard_map/ppermute | solution.py:960
  306.5 40.7 %collective-permute-start.25 = (f32[1,2304]{1,0:T(1,128)S(1)}, f32[1,2304]{1,0:T(1,128)S(1)}, u32[]{:S(2)}, u32[]{:S(2)}) collective-permute-start(f32[1,2304]{1,0:T(1,128)S(1)} %slice_add_fusion), channel_id=1, source_target_pairs={{0,8},{4,12},{8,0},{12,4},{16,24},{20,28},{24,16},{28,20},{1,9},{5... | collective-permute-start | bytes 27656 | tf_op jit(solution)/shard_map/ppermute | solution.py:960
  347.2 25.1 %collective-permute-start.39 = (bf16[4,648,128]{2,1,0:T(8,128)(2,1)}, bf16[4,648,128]{2,1,0:T(8,128)(2,1)S(1)}, u32[]{:S(2)}, u32[]{:S(2)}) collective-permute-start(bf16[4,648,128]{2,1,0:T(8,128)(2,1)} %get-tuple-element.192), channel_id=1, source_target_pairs={{0,8},{4,12},{8,0},{12,4},{16,24},{20,28},{24,16},{28,20},{1,9},{5... | collective-permute-start | bytes 1990664 | tf_op jit(solution)/shard_map/ppermute | solution.py:960
  348.7 43.1 %collective-permute-start.40 = (bf16[4,648,128]{2,1,0:T(8,128)(2,1)}, bf16[4,648,128]{2,1,0:T(8,128)(2,1)S(1)}, u32[]{:S(2)}, u32[]{:S(2)}) collective-permute-start(bf16[4,648,128]{2,1,0:T(8,128)(2,1)} %get-tuple-element.194), channel_id=1, source_target_pairs={{0,8},{4,12},{8,0},{12,4},{16,24},{20,28},{24,16},{28,20},{1,9},{5... | collective-permute-start | bytes 1990664 | tf_op jit(solution)/shard_map/ppermute | solution.py:960
  349.2 49.3 %collective-permute-start.6 = (bf16[2,2,4,8,1152]{4,3,2,1,0:T(8,128)(2,1)}, bf16[2,2,4,8,1152]{4,3,2,1,0:T(8,128)(2,1)S(1)}, u32[]{:S(2)}, u32[]{:S(2)}) collective-permute-start(bf16[2,2,4,8,1152]{4,3,2,1,0:T(8,128)(2,1)} %get-tuple-element.119), channel_id=1, source_target_pairs={{0,1},{1,0},{2,3},{3,2},{4,5},{5,4},{6,7},{7,6},{8,9},{9,8},{10,11... | collective-permute-start | bytes 884744 | tf_op jit(solution)/shard_map/ppermute | solution.py:384
  350.8 48.6 %collective-permute-start.7 = (bf16[2,2,4,8,1152]{4,3,2,1,0:T(8,128)(2,1)}, bf16[2,2,4,8,1152]{4,3,2,1,0:T(8,128)(2,1)S(1)}, u32[]{:S(2)}, u32[]{:S(2)}) collective-permute-start(bf16[2,2,4,8,1152]{4,3,2,1,0:T(8,128)(2,1)} %get-tuple-element.120), channel_id=1, source_target_pairs={{0,2},{1,3},{2,0},{3,1},{4,6},{5,7},{6,4},{7,5},{8,10},{9,11},{10,... | collective-permute-start | bytes 884744 | tf_op jit(solution)/shard_map/ppermute | solution.py:384
  354.7 46.7 %collective-permute-start.32 = (bf16[2,648,128]{2,1,0:T(8,128)(2,1)}, bf16[2,648,128]{2,1,0:T(8,128)(2,1)S(1)}, u32[]{:S(2)}, u32[]{:S(2)}) collective-permute-start(bf16[2,648,128]{2,1,0:T(8,128)(2,1)} %get-tuple-element.178), channel_id=1, source_target_pairs={{0,16},{4,20},{8,24},{12,28},{16,0},{20,4},{24,8},{28,12},{1,17},{... | collective-permute-start | bytes 995336 | tf_op jit(solution)/shard_map/ppermute | solution.py:960
  372.3 19.6 %copy-start.7 = (bf16[4,648,128]{2,1,0:T(8,128)(2,1)}, bf16[4,648,128]{2,1,0:T(8,128)(2,1)S(1)}, u32[]{:S(2)}) copy-start(bf16[4,648,128]{2,1,0:T(8,128)(2,1)S(1)} %collective-permute-done.39.refs_2_.refs_3_) | copy-start | bytes 1990660
  372.3 77.8 %collective-permute-start.20 = (bf16[2,672,128]{2,1,0:T(8,128)(2,1)}, bf16[2,672,128]{2,1,0:T(8,128)(2,1)S(1)}, u32[]{:S(2)}, u32[]{:S(2)}) collective-permute-start(bf16[2,672,128]{2,1,0:T(8,128)(2,1)} %get-tuple-element.157), channel_id=1, source_target_pairs={{0,16},{4,20},{8,24},{12,28},{16,0},{20,4},{24,8},{28,12},{1,17},{... | collective-permute-start | bytes 1032200 | tf_op jit(solution)/shard_map/ppermute | solution.py:960
  391.9 4.6 collective-permute-start.26
  392.7 8.7 %copy-start.39 = (bf16[2,672,128]{2,1,0:T(8,128)(2,1)S(1)}, bf16[2,672,128]{2,1,0:T(8,128)(2,1)}, u32[]{:S(2)}) copy-start(bf16[2,672,128]{2,1,0:T(8,128)(2,1)} %get-tuple-element.159) | copy-start | bytes 1032196
  396.4 38.5 %collective-permute-start.33 = (bf16[2,648,128]{2,1,0:T(8,128)(2,1)S(1)}, bf16[2,648,128]{2,1,0:T(8,128)(2,1)S(1)}, u32[]{:S(2)}, u32[]{:S(2)}) collective-permute-start(bf16[2,648,128]{2,1,0:T(8,128)(2,1)S(1)} %copy-done.40), channel_id=1, source_target_pairs={{0,16},{4,20},{8,24},{12,28},{16,0},{20,4},{24,8},{28,12},{1,17},{... | collective-permute-start | bytes 995336 | tf_op jit(solution)/shard_map/ppermute | solution.py:960
  398.5 57.6 %copy-start.15 = (bf16[2,2,4,8,1152]{4,3,2,1,0:T(8,128)(2,1)}, bf16[2,2,4,8,1152]{4,3,2,1,0:T(8,128)(2,1)S(1)}, u32[]{:S(2)}) copy-start(bf16[2,2,4,8,1152]{4,3,2,1,0:T(8,128)(2,1)S(1)} %collective-permute-done.6.refs_1_) | copy-start | bytes 884740
  398.5 43.6 %collective-permute-start.41 = (bf16[2,648,128]{2,1,0:T(8,128)(2,1)}, bf16[2,648,128]{2,1,0:T(8,128)(2,1)S(1)}, u32[]{:S(2)}, u32[]{:S(2)}) collective-permute-start(bf16[2,648,128]{2,1,0:T(8,128)(2,1)} %get-tuple-element.196), channel_id=1, source_target_pairs={{0,16},{4,20},{8,24},{12,28},{16,0},{20,4},{24,8},{28,12},{1,17},{... | collective-permute-start | bytes 995336 | tf_op jit(solution)/shard_map/ppermute | solution.py:960
  399.4 56.7 %copy-start.16 = (bf16[2,2,4,8,1152]{4,3,2,1,0:T(8,128)(2,1)}, bf16[2,2,4,8,1152]{4,3,2,1,0:T(8,128)(2,1)S(1)}, u32[]{:S(2)}) copy-start(bf16[2,2,4,8,1152]{4,3,2,1,0:T(8,128)(2,1)S(1)} %collective-permute-done.7.refs_2_) | copy-start | bytes 884740
  399.4 49.8 %collective-permute-start.42 = (bf16[2,648,128]{2,1,0:T(8,128)(2,1)}, bf16[2,648,128]{2,1,0:T(8,128)(2,1)S(1)}, u32[]{:S(2)}, u32[]{:S(2)}) collective-permute-start(bf16[2,648,128]{2,1,0:T(8,128)(2,1)} %get-tuple-element.198), channel_id=1, source_target_pairs={{0,16},{4,20},{8,24},{12,28},{16,0},{20,4},{24,8},{28,12},{1,17},{... | collective-permute-start | bytes 995336 | tf_op jit(solution)/shard_map/ppermute | solution.py:960
  401.4 50.8 %copy-start.11 = (bf16[2,648,128]{2,1,0:T(8,128)(2,1)}, bf16[2,648,128]{2,1,0:T(8,128)(2,1)S(1)}, u32[]{:S(2)}) copy-start(bf16[2,648,128]{2,1,0:T(8,128)(2,1)S(1)} %collective-permute-done.32.refs_2_.refs_3_) | copy-start | bytes 995332
  401.4 54.7 %collective-permute-start.21 = (bf16[2,672,128]{2,1,0:T(8,128)(2,1)S(1)}, bf16[2,672,128]{2,1,0:T(8,128)(2,1)S(1)}, u32[]{:S(2)}, u32[]{:S(2)}) collective-permute-start(bf16[2,672,128]{2,1,0:T(8,128)(2,1)S(1)} %copy-done.39), channel_id=1, source_target_pairs={{0,16},{4,20},{8,24},{12,28},{16,0},{20,4},{24,8},{28,12},{1,17},{... | collective-permute-start | bytes 1032200 | tf_op jit(solution)/shard_map/ppermute | solution.py:960
  434.9 17.3 %copy-start.14 = (bf16[2,648,128]{2,1,0:T(8,128)(2,1)}, bf16[2,648,128]{2,1,0:T(8,128)(2,1)S(1)}, u32[]{:S(2)}) copy-start(bf16[2,648,128]{2,1,0:T(8,128)(2,1)S(1)} %collective-permute-done.33.refs_6_.refs_7_) | copy-start | bytes 995332
  434.9 29.7 %collective-permute-start.8 = (bf16[2,2,4,8,1152]{4,3,2,1,0:T(8,128)(2,1)}, bf16[2,2,4,8,1152]{4,3,2,1,0:T(8,128)(2,1)S(1)}, u32[]{:S(2)}, u32[]{:S(2)}) collective-permute-start(bf16[2,2,4,8,1152]{4,3,2,1,0:T(8,128)(2,1)} %get-tuple-element.121), channel_id=1, source_target_pairs={{0,3},{1,2},{2,1},{3,0},{4,7},{5,6},{6,5},{7,4},{8,11},{9,10},{10,... | collective-permute-start | bytes 884744 | tf_op jit(solution)/shard_map/ppermute | solution.py:384
  442.0 15.8 %copy-start.12 = (bf16[2,648,128]{2,1,0:T(8,128)(2,1)}, bf16[2,648,128]{2,1,0:T(8,128)(2,1)S(1)}, u32[]{:S(2)}) copy-start(bf16[2,648,128]{2,1,0:T(8,128)(2,1)S(1)} %collective-permute-done.41.refs_2_.refs_3_) | copy-start | bytes 995332
  442.1 23.7 %collective-permute-start.9 = (bf16[2,2,4,8,1152]{4,3,2,1,0:T(8,128)(2,1)}, bf16[2,2,4,8,1152]{4,3,2,1,0:T(8,128)(2,1)S(1)}, u32[]{:S(2)}, u32[]{:S(2)}) collective-permute-start(bf16[2,2,4,8,1152]{4,3,2,1,0:T(8,128)(2,1)} %get-tuple-element.133), channel_id=1, source_target_pairs={{0,1},{1,0},{2,3},{3,2},{4,5},{5,4},{6,7},{7,6},{8,9},{9,8},{10,11... | collective-permute-start | bytes 884744 | tf_op jit(solution)/shard_map/ppermute | solution.py:384
  449.2 8.7 %copy-start.13 = (bf16[2,648,128]{2,1,0:T(8,128)(2,1)}, bf16[2,648,128]{2,1,0:T(8,128)(2,1)S(1)}, u32[]{:S(2)}) copy-start(bf16[2,648,128]{2,1,0:T(8,128)(2,1)S(1)} %collective-permute-done.42.refs_6_.refs_7_) | copy-start | bytes 995332
  449.2 18.3 %collective-permute-start.10 = (bf16[2,2,4,8,1152]{4,3,2,1,0:T(8,128)(2,1)}, bf16[2,2,4,8,1152]{4,3,2,1,0:T(8,128)(2,1)S(1)}, u32[]{:S(2)}, u32[]{:S(2)}) collective-permute-start(bf16[2,2,4,8,1152]{4,3,2,1,0:T(8,128)(2,1)} %get-tuple-element.134), channel_id=1, source_target_pairs={{0,2},{1,3},{2,0},{3,1},{4,6},{5,7},{6,4},{7,5},{8,10},{9,11},{10,... | collective-permute-start | bytes 884744 | tf_op jit(solution)/shard_map/ppermute | solution.py:384
  450.1 8.4 %copy-start.9 = (bf16[2,672,128]{2,1,0:T(8,128)(2,1)}, bf16[2,672,128]{2,1,0:T(8,128)(2,1)S(1)}, u32[]{:S(2)}) copy-start(bf16[2,672,128]{2,1,0:T(8,128)(2,1)S(1)} %collective-permute-done.20.refs_2_.refs_3_) | copy-start | bytes 1032196
  450.1 17.8 %collective-permute-start.11 = (bf16[2,2,4,8,1152]{4,3,2,1,0:T(8,128)(2,1)}, bf16[2,2,4,8,1152]{4,3,2,1,0:T(8,128)(2,1)S(1)}, u32[]{:S(2)}, u32[]{:S(2)}) collective-permute-start(bf16[2,2,4,8,1152]{4,3,2,1,0:T(8,128)(2,1)} %get-tuple-element.135), channel_id=1, source_target_pairs={{0,3},{1,2},{2,1},{3,0},{4,7},{5,6},{6,5},{7,4},{8,11},{9,10},{10,... | collective-permute-start | bytes 884744 | tf_op jit(solution)/shard_map/ppermute | solution.py:384
  456.1 12.8 %collective-permute-start.34 = (bf16[1,648,128]{2,1,0:T(8,128)(2,1)}, bf16[1,648,128]{2,1,0:T(8,128)(2,1)S(1)}, u32[]{:S(2)}, u32[]{:S(2)}) collective-permute-start(bf16[1,648,128]{2,1,0:T(8,128)(2,1)} %get-tuple-element.183), channel_id=1, source_target_pairs={{0,2},{1,3},{2,0},{3,1},{4,6},{5,7},{6,4},{7,5},{8,10},{9,11},{10,... | collective-permute-start | bytes 497672 | tf_op jit(solution)/shard_map/ppermute | solution.py:960
  464.6 11.0 %collective-permute-start.35 = (bf16[1,648,128]{2,1,0:T(8,128)(2,1)S(1)}, bf16[1,648,128]{2,1,0:T(8,128)(2,1)S(1)}, u32[]{:S(2)}, u32[]{:S(2)}) collective-permute-start(bf16[1,648,128]{2,1,0:T(8,128)(2,1)S(1)} %copy-done.47), channel_id=1, source_target_pairs={{0,1},{1,0},{2,3},{3,2},{4,5},{5,4},{6,7},{7,6},{8,9},{9,8},{10,11... | collective-permute-start | bytes 497672 | tf_op jit(solution)/shard_map/ppermute | solution.py:960
  465.7 7.7 %copy-start.18 = (bf16[2,2,4,8,1152]{4,3,2,1,0:T(8,128)(2,1)}, bf16[2,2,4,8,1152]{4,3,2,1,0:T(8,128)(2,1)S(1)}, u32[]{:S(2)}) copy-start(bf16[2,2,4,8,1152]{4,3,2,1,0:T(8,128)(2,1)S(1)} %collective-permute-done.9.refs_1_) | copy-start | bytes 884740
  465.7 12.7 %collective-permute-start.43 = (bf16[1,648,128]{2,1,0:T(8,128)(2,1)S(1)}, bf16[1,648,128]{2,1,0:T(8,128)(2,1)S(1)}, u32[]{:S(2)}, u32[]{:S(2)}) collective-permute-start(bf16[1,648,128]{2,1,0:T(8,128)(2,1)S(1)} %copy-done.49), channel_id=1, source_target_pairs={{0,2},{1,3},{2,0},{3,1},{4,6},{5,7},{6,4},{7,5},{8,10},{9,11},{10,... | collective-permute-start | bytes 497672 | tf_op jit(solution)/shard_map/ppermute | solution.py:960
  467.5 10.9 %collective-permute-start.44 = (bf16[1,648,128]{2,1,0:T(8,128)(2,1)S(1)}, bf16[1,648,128]{2,1,0:T(8,128)(2,1)S(1)}, u32[]{:S(2)}, u32[]{:S(2)}) collective-permute-start(bf16[1,648,128]{2,1,0:T(8,128)(2,1)S(1)} %copy-done.48), channel_id=1, source_target_pairs={{0,1},{1,0},{2,3},{3,2},{4,5},{5,4},{6,7},{7,6},{8,9},{9,8},{10,11... | collective-permute-start | bytes 497672 | tf_op jit(solution)/shard_map/ppermute | solution.py:960
  467.9 15.8 %collective-permute-start.22 = (bf16[1,672,128]{2,1,0:T(8,128)(2,1)}, bf16[1,672,128]{2,1,0:T(8,128)(2,1)S(1)}, u32[]{:S(2)}, u32[]{:S(2)}) collective-permute-start(bf16[1,672,128]{2,1,0:T(8,128)(2,1)} %get-tuple-element.162), channel_id=1, source_target_pairs={{0,2},{1,3},{2,0},{3,1},{4,6},{5,7},{6,4},{7,5},{8,10},{9,11},{10,... | collective-permute-start | bytes 516104 | tf_op jit(solution)/shard_map/ppermute | solution.py:960
  468.9 14.8 %collective-permute-start.23 = (bf16[1,672,128]{2,1,0:T(8,128)(2,1)}, bf16[1,672,128]{2,1,0:T(8,128)(2,1)S(1)}, u32[]{:S(2)}, u32[]{:S(2)}) collective-permute-start(bf16[1,672,128]{2,1,0:T(8,128)(2,1)} %get-tuple-element.163), channel_id=1, source_target_pairs={{0,1},{1,0},{2,3},{3,2},{4,5},{5,4},{6,7},{7,6},{8,9},{9,8},{10,11... | collective-permute-start | bytes 516104 | tf_op jit(solution)/shard_map/ppermute | solution.py:960
  (31 other events, 101.7 us)
